TPU v7x, 512 devices: a whole 4x8x8 slice. The times are simulated.
512 devices in a mesh: row: 16 (over y, core), col: 32 (over x, z).
Axes of the slice: x: 4, y: 8, z: 8, core: 2. Of those that a mesh axis runs over, the one named last changes fastest.
Arguments:
- demand: bfloat16 [196608, 128], P(('row', 'col')), may hold values from -6 to 6
- tile_data: bfloat16 [16, 32, 128, 128, 128], P('row', 'col'), may hold values from -0.078125 to 0.078125
- tile_row: int32 [16, 32, 128], P('row', 'col'), may hold values from 0 to 48, as said below
- tile_col: int32 [16, 32, 128], P('row', 'col'), may hold values from 0 to 95, as said below
Outputs:
- leontief: bfloat16 [196608, 128], P(('row', 'col'))
Inputs may be any that keep to these rules, and one draw needn't show every extreme that they name: `tile_row`: the value 16 * 3 marks an empty slot. In every index pair the live slots come first and number at least 42; in every draw some index pair has all 128 slots live. Two slots may name the same tile position; their tiles then add. `tile_col`: empty slots carry a column too, which is ignored.
All inputs are finite; a program needn't handle non-finite values.
Results may differ from a plain program's by a relative error of at most 0.018.
Values may be sent and summed in bfloat16 or wider, within the bound.
No kernel may reach another device: no remote copies, remote signals or barrier semaphores. Data moves between devices by JAX's collectives and lax.ppermute only.
A program may use at most 64 MiB of HBM per device.

v0:
```python
import jax
import jax.numpy as jnp
from jax import lax
from jax.sharding import Mesh
from jax.sharding import PartitionSpec as P

COL = ("col_0", "col_1")
ROW_COL = ("row", "col_0", "col_1")


def in_order(blocks, dim):
    shape = list(blocks.shape[1:])
    shape[dim] *= blocks.shape[0]
    return jnp.moveaxis(blocks, 0, dim).reshape(shape)


def gather_in_order(array, axes, order):
    blocks = array[None]
    for k in order:
        blocks = lax.all_gather(blocks, axes[k], axis=0, tiled=True)
    held = [lax.axis_size(axes[k]) for k in reversed(order)]
    blocks = blocks.reshape(*held, *array.shape)
    turned = sorted(range(len(order)), key=lambda place: order[len(order) - 1 - place])
    return blocks.transpose(*turned, *range(len(order), blocks.ndim)).reshape(-1, *array.shape)


def gather_axes(array, axes, order, dim):
    return in_order(gather_in_order(array, axes, order), dim)


def cut_along(array, dim, devices):
    shape = array.shape
    blocks = array.reshape(*shape[:dim], devices, shape[dim] // devices, *shape[dim + 1 :])
    return jnp.moveaxis(blocks, dim, 0)


def summed_on_arrival(array, axis, dim):
    blocks = cut_along(array, dim, lax.axis_size(axis))
    arrived = lax.all_to_all(blocks, axis, split_axis=0, concat_axis=0, tiled=True)
    return arrived.astype(jnp.float32).sum(axis=0)


def multiply(panel_piece, tile_block, slot_rows, slot_cols):
    edge = tile_block.shape[-1]
    columns = panel_piece.shape[1]
    slot_count = tile_block.shape[0]
    local_rows = lax.axis_size("row") * (panel_piece.shape[0] // edge)
    gathered = gather_axes(panel_piece, COL, (0, 1), 0)
    blocks = gathered.reshape(-1, edge, columns)
    picked = jnp.take(blocks, slot_cols, axis=0)
    products = jnp.einsum("stk,skc->stc", tile_block, picked, preferred_element_type=jnp.float32)
    products = products.reshape(slot_count, -1)
    upper = products.astype(jnp.bfloat16)
    lower = (products - upper.astype(jnp.float32)).astype(jnp.bfloat16)
    targets = jnp.arange(local_rows, dtype=jnp.int32)
    onehot = (slot_rows[None, :] == targets[:, None]).astype(jnp.bfloat16)
    partial_value = jnp.dot(onehot, upper, preferred_element_type=jnp.float32)
    partial_value = partial_value + jnp.dot(onehot, lower, preferred_element_type=jnp.float32)
    partial_value = lax.optimization_barrier(partial_value.astype(jnp.bfloat16)).astype(jnp.float32)
    partial_value = partial_value.reshape(local_rows * edge, columns)
    summed = summed_on_arrival(partial_value.astype(jnp.bfloat16), "row", 0)
    return summed.astype(jnp.bfloat16)


def body(demand, tile_data, tile_row, tile_col):
    tile_block = tile_data[0, 0]
    slot_rows = tile_row[0, 0]
    slot_cols = tile_col[0, 0]
    first_term = multiply(demand, tile_block, slot_rows, slot_cols)
    second_term = multiply(first_term, tile_block, slot_rows, slot_cols)
    summed = (
        demand.astype(jnp.float32)
        + first_term.astype(jnp.float32)
        + second_term.astype(jnp.float32)
    )
    return summed.astype(jnp.bfloat16)


def solution(mesh):
    torus = Mesh(mesh.devices.reshape(mesh.shape["row"], 4, 8), ("row", "col_0", "col_1"))
    return jax.shard_map(
        body,
        mesh=torus,
        in_specs=(
            P(ROW_COL, None),
            P("row", COL, None, None, None),
            P("row", COL, None),
            P("row", COL, None),
        ),
        out_specs=P(ROW_COL, None),
        check_vma=False,
    )
```

profile of v0, /device:TPU:1, one launch (start us, length us, event | category | flops | bytes accessed | tf_op | source)
XLA Modules:
  0.0 296.3 jit_solution(10210878075228454600)
XLA Ops:
  6.5 0.0 all-gather.5.cloned.1.call-start
  6.5 13.0 %all-gather = bf16[1536,128]{1,0:T(8,128)(2,1)} all-gather(bf16[384,128]{1,0:T(8,128)(2,1)} %param.6), channel_id=2, replica_groups=mesh['row'=16,'col_0'=4,'col_1'=8] {'col_0'}, dimensions={0}, use_global_device_ids=true | all-gather | bytes 491520 | tf_op jit(solution)/shard_map/all_gather | solution.py:20
  19.5 0.0 all-gather.5.cloned.1.call-update
  19.5 0.0 all-gather.7.cloned.1.call-start
  19.6 0.7 compare_select_fusion
  20.2 0.7 compare_and_fusion
  20.9 52.9 %all-gather.5.cloned.1.call-done = bf16[32,384,128]{2,1,0:T(8,128)(2,1)} async-done(((bf16[4,384,128]{2,1,0:T(8,128)(2,1)}), bf16[32,384,128]{2,1,0:T(8,128)(2,1)}) %all-gather.5.cloned.1.call-update) | async-done | bytes 3145744 | tf_op jit(solution)/shard_map/all_gather | solution.py:20
  73.8 2.1 copy.15
  76.0 3.0 %gather_fusion = bf16[128,128,128]{2,1,0:T(8,128)(2,1)} fusion(bf16[96,128,128]{2,1,0:T(8,128)(2,1)S(1)} %bitcast.45, s32[1024]{0:T(1024)S(1)} %pad_clamp_fusion), kind=kCustom, calls=%fused_computation.clone | custom fusion | bytes 8389120 | tf_op jit(solution)/shard_map/jit(_take)/gather | solution.py:50
  79.0 9.9 %fusion.12 = f32[128,128,128]{1,2,0:T(8,128)} fusion(bf16[1,1,128,128,128]{4,3,2,1,0:T(8,128)(2,1)} %param.7, bf16[128,128,128]{2,1,0:T(8,128)(2,1)} %gather_fusion, pred[128]{0:T(512)(128)(4,1)S(1)} %compare_and_fusion), kind=kOutput, calls=%fused_computation.20 | convolution fusion | flops 538968064 | bytes 16777344 | tf_op jit(solution)/shard_map/stk,skc->stc/dot_general | solution.py:51
  88.9 9.4 %copy.17 = f32[128,128,128]{0,2,1:T(8,128)} copy(f32[128,128,128]{1,2,0:T(8,128)} %fusion.12) | data formatting | bytes 16777216 | tf_op jit(solution)/shard_map/stk,skc->stc/dot_general | solution.py:51
  98.3 0.0 copy-start.1
  98.3 4.0 %fusion.3 = (bf16[128,16384]{0,1:T(8,128)(2,1)S(1)}, bf16[128,16384]{0,1:T(8,128)(2,1)S(1)}) fusion(f32[128,128,128]{0,2,1:T(8,128)} %copy.17), kind=kLoop, calls=%fused_computation.11 | loop fusion | flops 8388608 | bytes 16777216 | tf_op jit(solution)/shard_map/convert_element_type | solution.py:54
  102.3 0.0 copy-done.1
  102.4 1.5 fusion.25
  103.9 1.5 fusion
  105.5 0.8 convert_element_type.59
  106.2 47.0 %all_to_all.10 = bf16[16,384,128]{2,1,0:T(8,128)(2,1)S(1)} all-to-all(bf16[16,384,128]{2,1,0:T(8,128)(2,1)S(1)} %convert_element_type.59), channel_id=1, replica_groups=mesh['row'=16,'col_0'=4,'col_1'=8] {'row'}, dimensions={0} | all-to-all | bytes 3145728 | tf_op jit(solution)/shard_map/all_to_all | solution.py:39
  153.2 0.2 reduce_sum.24
  153.4 11.9 %all-gather.1 = bf16[1536,128]{1,0:T(8,128)(2,1)} all-gather(bf16[384,128]{1,0:T(8,128)(2,1)S(1)} %reduce_sum.24), channel_id=3, replica_groups=mesh['row'=16,'col_0'=4,'col_1'=8] {'col_0'}, dimensions={0}, use_global_device_ids=true | all-gather | bytes 491520 | tf_op jit(solution)/shard_map/all_gather | solution.py:20
  165.4 0.0 all-gather.7.cloned.1.call-update
  165.4 43.8 %all-gather.7.cloned.1.call-done = bf16[32,384,128]{2,1,0:T(8,128)(2,1)} async-done(((bf16[4,384,128]{2,1,0:T(8,128)(2,1)}), bf16[32,384,128]{2,1,0:T(8,128)(2,1)}) %all-gather.7.cloned.1.call-update) | async-done | bytes 3145744 | tf_op jit(solution)/shard_map/all_gather | solution.py:20
  209.2 2.1 copy.18
  211.3 3.0 %gather_fusion.1 = bf16[128,128,128]{2,1,0:T(8,128)(2,1)} fusion(bf16[96,128,128]{2,1,0:T(8,128)(2,1)S(1)} %bitcast.44, s32[1024]{0:T(1024)S(1)} %pad_clamp_fusion), kind=kCustom, calls=%fused_computation.1.clone | custom fusion | bytes 8389120 | tf_op jit(solution)/shard_map/jit(_take)/gather | solution.py:50
  214.4 9.9 %fusion.17 = f32[128,128,128]{1,2,0:T(8,128)} fusion(bf16[1,1,128,128,128]{4,3,2,1,0:T(8,128)(2,1)} %param.7, bf16[128,128,128]{2,1,0:T(8,128)(2,1)} %gather_fusion.1, pred[128]{0:T(512)(128)(4,1)S(1)} %compare_and_fusion), kind=kOutput, calls=%fused_computation.21 | convolution fusion | flops 538968064 | bytes 16777344 | tf_op jit(solution)/shard_map/stk,skc->stc/dot_general | solution.py:51
  224.3 9.4 %copy.20 = f32[128,128,128]{0,2,1:T(8,128)} copy(f32[128,128,128]{1,2,0:T(8,128)} %fusion.17) | data formatting | bytes 16777216 | tf_op jit(solution)/shard_map/stk,skc->stc/dot_general | solution.py:51
  233.7 4.0 %fusion.2 = (bf16[128,16384]{0,1:T(8,128)(2,1)S(1)}, bf16[128,16384]{0,1:T(8,128)(2,1)S(1)}) fusion(f32[128,128,128]{0,2,1:T(8,128)} %copy.20), kind=kLoop, calls=%fused_computation.8 | loop fusion | flops 8388608 | bytes 16777216 | tf_op jit(solution)/shard_map/convert_element_type | solution.py:54
  237.7 1.5 fusion.24
  239.3 1.5 fusion.1
  240.8 0.0 copy-start
  240.8 0.8 convert_element_type.65
  241.6 47.0 %all_to_all.11 = bf16[16,384,128]{2,1,0:T(8,128)(2,1)S(1)} all-to-all(bf16[16,384,128]{2,1,0:T(8,128)(2,1)S(1)} %convert_element_type.65), channel_id=1, replica_groups=mesh['row'=16,'col_0'=4,'col_1'=8] {'row'}, dimensions={0} | all-to-all | bytes 3145728 | tf_op jit(solution)/shard_map/all_to_all | solution.py:39
  288.6 0.2 reduce_sum.25
  288.8 0.0 copy-done
  288.8 0.7 add_convert_fusion
  (1 shorter events, 0.0 us)
Async XLA Ops:
  6.5 67.3 %all-gather.5.cloned.1.call-start = ((), (), s32[]{:S(2)}) async-start(), calls=%async_computation.2 | async-start | bytes 3538944 | tf_op jit(solution)/shard_map/all_gather | solution.py:20
  19.5 189.7 %all-gather.7.cloned.1.call-start = ((), (), s32[]{:S(2)}) async-start(), calls=%async_computation.3 | async-start | bytes 3538944 | tf_op jit(solution)/shard_map/all_gather | solution.py:20
  98.3 4.0 %copy-start.1 = (s32[1,1,128]{2,1,0:T(1,128)S(1)}, s32[1,1,128]{2,1,0:T(1,128)}, u32[]{:S(2)}) copy-start(s32[1,1,128]{2,1,0:T(1,128)} %param.8) | copy-start | bytes 1540
  240.8 48.0 %copy-start = (bf16[384,128]{1,0:T(8,128)(2,1)S(1)}, bf16[384,128]{1,0:T(8,128)(2,1)}, u32[]{:S(2)}) copy-start(bf16[384,128]{1,0:T(8,128)(2,1)} %param.6) | copy-start | bytes 294916
Sparse Core Ops, SparseCore 0:
  19.6 54.1 all-gather.4
  165.5 43.6 all-gather.6
where the time goes:
time: 297 us; the launch traced here: 296 us
  blocking collectives  119 us (40%)
  waiting for transfers between devices  96.8 us (33%)
  local copies, waits for them, and re-layouts  30.6 us (10%)
  matrix products  26 us (9%)
  between operations  13.5 us (5%)
  other arithmetic  10.5 us (4%)
    all_gather x2, waiting for transfers between devices, gather_in_order(): blocks = lax.all_gather(blocks, axes[k], axis=0, tiled=True)  96.8 us
    all_to_all x2, blocking collectives, summed_on_arrival(): lax.all_to_all(blocks, axis, split_axis=0, concat_axis=0, tiled=True)  94 us
    all_gather x2, blocking collectives, gather_in_order(): blocks = lax.all_gather(blocks, axes[k], axis=0, tiled=True)  24.9 us
    dot_general x2, matrix products, multiply(): jnp.einsum('stk,skc->stc', tile_block, picked, preferred_element_type=jnp...  19.8 us
    dot_general x2, local copies, waits for them, and re-layouts, multiply(): jnp.einsum('stk,skc->stc', tile_block, picked, preferred_element_type=jnp...  18.8 us
    convert_element_type x2, other arithmetic, multiply(): lower = (products - upper.astype(jnp.float32)).astype(jnp.bfloat16)  8.06 us
    gather x2, local copies, waits for them, and re-layouts, multiply(): picked = jnp.take(blocks, slot_cols, axis=0)  6.05 us
  transfers between devices with their start and end apart: 2, of which 2 were waited for; matrix products, arithmetic and copies ran while one was open for 0% of the time, Pallas kernels for 0%

commit v1 on v0

v1 whole, which is shorter than its diff:
```python
import jax
import jax.numpy as jnp
from jax import lax
from jax.experimental import pallas as pl
from jax.experimental.pallas import tpu as pltpu
from jax.sharding import Mesh
from jax.sharding import PartitionSpec as P

COL = ("x", "z")
ROW_COL = ("y", "core", "x", "z")
CHUNK = 16


def spread(piece, axis):
    copies = jnp.broadcast_to(piece[None], (lax.axis_size(axis), *piece.shape))
    return lax.all_to_all(copies, axis, split_axis=0, concat_axis=0, tiled=True)


def gather_panel(piece):
    along_z = spread(piece, "z").reshape(-1, piece.shape[1])
    return spread(along_z, "x").reshape(-1, piece.shape[1])


def tile_kernel(spans, core_ref, rows_ref, cols_ref, tiles_ref, panel_ref, keep_ref, send_ref, total_ref):
    step = pl.program_id(0)
    edge = tiles_ref.shape[-1]
    span_tiles = keep_ref.shape[0] // (spans // 2 * edge)
    half = spans // 2 * span_tiles
    core = core_ref[0]

    @pl.when(step == 0)
    def _():
        total_ref[...] = jnp.zeros_like(total_ref)

    products = []
    places = []
    for slot in range(tiles_ref.shape[0]):
        col = cols_ref[step * tiles_ref.shape[0] + slot]
        block = panel_ref[pl.ds(pl.multiple_of(col * edge, edge), edge), :]
        products.append(jnp.dot(tiles_ref[slot], block, preferred_element_type=jnp.float32))
        row = rows_ref[step * tiles_ref.shape[0] + slot]
        span = row // span_tiles
        place = (span // 2) * span_tiles + row % span_tiles + half * lax.bitwise_xor(span % 2, core)
        places.append(jnp.where(row >= 2 * half, 2 * half, place))
    for product, place in zip(products, places):
        at = pl.ds(pl.multiple_of(place * edge, edge), edge)
        total_ref[at, :] += product

    @pl.when(step == pl.num_programs(0) - 1)
    def _():
        keep_ref[...] = total_ref[: half * edge].astype(keep_ref.dtype)
        send_ref[...] = total_ref[half * edge : 2 * half * edge].astype(send_ref.dtype)


def tile_products(panel, tile_block, slot_rows, slot_cols, core, spans, span_rows):
    slots, edge = tile_block.shape[0], tile_block.shape[-1]
    columns = panel.shape[1]
    half_rows = spans // 2 * span_rows
    chunk = min(CHUNK, slots)
    whole = pl.BlockSpec((half_rows, columns), lambda i, *_: (0, 0))
    return pl.pallas_call(
        lambda *refs: tile_kernel(spans, *refs),
        out_shape=[
            jax.ShapeDtypeStruct((half_rows, columns), jnp.float32),
            jax.ShapeDtypeStruct((half_rows, columns), jnp.bfloat16),
        ],
        grid_spec=pltpu.PrefetchScalarGridSpec(
            num_scalar_prefetch=3,
            grid=(slots // chunk,),
            in_specs=[
                pl.BlockSpec((chunk, edge, edge), lambda i, *_: (i, 0, 0)),
                pl.BlockSpec(panel.shape, lambda i, *_: (0, 0), pipeline_mode=pl.Buffered(1)),
            ],
            out_specs=[whole, whole],
            scratch_shapes=[pltpu.VMEM((2 * half_rows + edge, columns), jnp.float32)],
        ),
        compiler_params=pltpu.CompilerParams(
            dimension_semantics=("arbitrary",), vmem_limit_bytes=24 << 20
        ),
        cost_estimate=pl.CostEstimate(
            flops=2 * slots * edge * edge * columns,
            bytes_accessed=2 * slots * edge * edge + 2 * panel.size + 6 * half_rows * columns,
            transcendentals=0,
        ),
    )(core, slot_rows, slot_cols, tile_block, panel)


def multiply(piece, tile_block, slot_rows, slot_cols, core):
    columns = piece.shape[1]
    chips = lax.axis_size("y")
    panel = gather_panel(piece)
    keep, send = tile_products(
        panel, tile_block, slot_rows, slot_cols, core, 2 * chips, piece.shape[0]
    )
    other = lax.ppermute(send, "core", [(0, 1), (1, 0)])
    both = (keep + other.astype(jnp.float32)).astype(jnp.bfloat16)
    arrived = lax.all_to_all(
        both.reshape(chips, -1, columns), "y", split_axis=0, concat_axis=0, tiled=True
    )
    return arrived.astype(jnp.float32).sum(axis=0).astype(jnp.bfloat16)


def body(demand, tile_data, tile_row, tile_col):
    tile_block = tile_data[0, 0]
    slot_rows = tile_row[0, 0]
    slot_cols = tile_col[0, 0]
    core = lax.axis_index("core").astype(jnp.int32).reshape(1)
    first_term = multiply(demand, tile_block, slot_rows, slot_cols, core)
    second_term = multiply(first_term, tile_block, slot_rows, slot_cols, core)
    summed = (
        demand.astype(jnp.float32)
        + first_term.astype(jnp.float32)
        + second_term.astype(jnp.float32)
    )
    return summed.astype(jnp.bfloat16)


def solution(mesh):
    rows, cols = mesh.shape["row"], mesh.shape["col"]
    torus = Mesh(
        mesh.devices.reshape(rows // 2, 2, 4, cols // 4), ("y", "core", "x", "z")
    )
    return jax.shard_map(
        body,
        mesh=torus,
        in_specs=(
            P(ROW_COL, None),
            P(("y", "core"), COL, None, None, None),
            P(("y", "core"), COL, None),
            P(("y", "core"), COL, None),
        ),
        out_specs=P(ROW_COL, None),
        check_vma=False,
    )
```

time: 297 us -> 217 us (0.73)
  waiting for transfers between devices: 96.8 us -> 38.6 us
  matrix products: 26 us -> 0 us
  blocking collectives: 119 us -> 145 us
  local copies, waits for them, and re-layouts: 30.6 us -> 5.77 us
  starting transfers between devices: 0.04 us -> 16.4 us
  between operations: 13.5 us -> 0.09 us
  other arithmetic: 10.5 us -> 1.32 us
  Pallas kernels: 0 us -> 8.37 us
    all_gather x2 -> x0, waiting for transfers between devices: 96.8 us -> none  [gather_in_order(): blocks = lax.all_gather(blocks, axes[k], axis=0, tiled=True)]
    all_to_all x2 -> x5, blocking collectives: 94 us -> 145 us  [the longest x3 91.5 us: spread(): return lax.all_to_all(copies, axis, split_axis=0, concat_axis=0, tiled=True)]
    all_to_all x0 -> x1, waiting for transfers between devices: none -> 34.9 us  [spread(): return lax.all_to_all(copies, axis, split_axis=0, concat_axis=0, tiled=True)]
    dot_general x6 -> x0, matrix products: 26 us -> none  [the longest x2 19.8 us: multiply(): jnp.einsum('stk,skc->stc', tile_block, picked, preferred_element_type=jnp...]
    all_gather x2 -> x0, blocking collectives: 24.9 us -> none  [gather_in_order(): blocks = lax.all_gather(blocks, axes[k], axis=0, tiled=True)]
    dot_general x2 -> x0, local copies, waits for them, and re-layouts: 18.8 us -> none  [multiply(): jnp.einsum('stk,skc->stc', tile_block, picked, preferred_element_type=jnp...]
    ppermute x0 -> x2, starting transfers between devices: none -> 12.2 us  [multiply(): other = lax.ppermute(send, 'core', [(0, 1), (1, 0)])]
    pallas_call x0 -> x2, Pallas kernels: none -> 8.37 us  [tile_products(): pl.pallas_call(lambda *refs: tile_kernel(spans, *refs), out_shape=[jax.Sh...]
  transfers between devices with their start and end apart: 2 -> 3, of which waited for: 2 -> 3; matrix products, arithmetic and copies ran while one was open for 0% -> 0% of each run, Pallas kernels for 0% -> 0%
where the time goes in v1:
time: 217 us; the launch traced here: 216 us
  blocking collectives  145 us (67%)
  waiting for transfers between devices  38.6 us (18%)
  starting transfers between devices  16.4 us (8%)
  Pallas kernels  8.37 us (4%)
  local copies, waits for them, and re-layouts  5.77 us (3%)
    all_to_all x3, blocking collectives, spread(): return lax.all_to_all(copies, axis, split_axis=0, concat_axis=0, tiled=True)  91.5 us
    all_to_all x2, blocking collectives, multiply(): lax.all_to_all(both.reshape(chips, -1, columns), 'y', split_axis=0, conca...  54 us
    all_to_all x1, waiting for transfers between devices, spread(): return lax.all_to_all(copies, axis, split_axis=0, concat_axis=0, tiled=True)  34.9 us
    ppermute x2, starting transfers between devices, multiply(): other = lax.ppermute(send, 'core', [(0, 1), (1, 0)])  12.2 us
    pallas_call x2, Pallas kernels, tile_products(): pl.pallas_call(lambda *refs: tile_kernel(spans, *refs), out_shape=[jax.Sh...  8.37 us
  transfers between devices with their start and end apart: 3, of which 3 were waited for; matrix products, arithmetic and copies ran while one was open for 0% of the time, Pallas kernels for 0%

profile of v1, /device:TPU:1, one launch (start us, length us, event | category | flops | bytes accessed | tf_op | source)
XLA Modules:
  0.0 216.1 jit_solution(4986954896660641075)
XLA Ops:
  0.0 1.0 broadcast_in_dim.12
  1.0 32.3 %all_to_all.30 = bf16[8,384,128]{2,1,0:T(8,128)(2,1)S(1)} all-to-all(bf16[8,384,128]{2,1,0:T(8,128)(2,1)S(1)} %broadcast_in_dim.12), channel_id=1, replica_groups=mesh['y'=8,'core'=2,'x'=4,'z'=8] {'z'}, dimensions={0} | all-to-all | bytes 1572864 | tf_op jit(solution)/shard_map/all_to_all | solution.py:16
  33.3 2.1 broadcast_in_dim.28
  35.3 0.0 copy-start.2
  35.3 0.0 copy-start.3
  35.3 4.1 %all-to-all-start.1 = ((bf16[4,3072,128]{2,1,0:T(8,128)(2,1)}), bf16[4,3072,128]{2,1,0:T(8,128)(2,1)S(1)}, u32[]{:S(2)}, u32[]{:S(2)}) async-start(bf16[4,3072,128]{2,1,0:T(8,128)(2,1)} %broadcast_in_dim.28), calls=%async_computation.1 | async-start | bytes 6291456 | tf_op jit(solution)/shard_map/all_to_all | solution.py:16
  39.5 34.9 %all-to-all-done.1 = bf16[4,3072,128]{2,1,0:T(8,128)(2,1)S(1)} async-done(((bf16[4,3072,128]{2,1,0:T(8,128)(2,1)}), bf16[4,3072,128]{2,1,0:T(8,128)(2,1)S(1)}, u32[]{:S(2)}, u32[]{:S(2)}) %all-to-all-start.1) | async-done | bytes 3145760 | tf_op jit(solution)/shard_map/all_to_all | solution.py:16
  74.3 0.0 copy-done.2
  74.3 0.0 copy-done.3
  74.3 0.0 copy-start
  74.4 2.2 %copy-done = bf16[1,1,128,128,128]{4,3,2,1,0:T(8,128)(2,1)S(1)} copy-done((bf16[1,1,128,128,128]{4,3,2,1,0:T(8,128)(2,1)S(1)}, bf16[1,1,128,128,128]{4,3,2,1,0:T(8,128)(2,1)}, u32[]{:S(2)}) %copy-start) | copy-done | bytes 4194328
  76.5 4.2 %shard_map.46 = (f32[3072,128]{1,0:T(8,128)S(1)}, bf16[3072,128]{1,0:T(8,128)(2,1)S(1)}) custom-call(s32[1]{0:T(128)} %bitcast.refs_0_, s32[128]{0:T(128)S(1)} %bitcast.14, s32[128]{0:T(128)S(1)} %bitcast.16, bf16[128,128,128]{2,1,0:T(8,128)(2,1)S(1)} %bitcast.10, bf16[12288,128]{1,0:T(8,128)(2,1)S(1)} %bitcast.12), custom_call_target="tpu_custom_call" | custom-call | flops 536870912 | bytes 9699328 | tf_op jit(solution)/shard_map/pallas_call | solution.py:61
  80.7 5.6 %collective-permute-start = (bf16[3072,128]{1,0:T(8,128)(2,1)S(1)}, bf16[3072,128]{1,0:T(8,128)(2,1)S(1)}, u32[]{:S(2)}, u32[]{:S(2)}) collective-permute-start(bf16[3072,128]{1,0:T(8,128)(2,1)S(1)} %get-tuple-element.10), channel_id=1, source_target_pairs={{0,32},{32,0},{1,33},{33,1},{2,34},{34,2},{3,35},{35,3},{4,36},{36... | collective-permute-start | bytes 2359304 | tf_op jit(solution)/shard_map/ppermute | solution.py:95
  86.3 1.9 collective-permute-done
  88.2 0.2 add_convert_fusion.1
  88.4 28.9 %all_to_all.31 = bf16[8,384,128]{2,1,0:T(8,128)(2,1)S(1)} all-to-all(bf16[8,384,128]{2,1,0:T(8,128)(2,1)S(1)} %bitcast.18), channel_id=1, replica_groups=mesh['y'=8,'core'=2,'x'=4,'z'=8] {'y'}, dimensions={0} | all-to-all | bytes 1572864 | tf_op jit(solution)/shard_map/all_to_all | solution.py:97
  117.3 0.1 reduce_sum.24
  117.5 0.1 broadcast_in_dim.29
  117.6 22.7 %all_to_all.32 = bf16[8,384,128]{2,1,0:T(8,128)(2,1)S(1)} all-to-all(bf16[8,384,128]{2,1,0:T(8,128)(2,1)S(1)} %broadcast_in_dim.29), channel_id=1, replica_groups=mesh['y'=8,'core'=2,'x'=4,'z'=8] {'z'}, dimensions={0} | all-to-all | bytes 1572864 | tf_op jit(solution)/shard_map/all_to_all | solution.py:16
  140.2 0.4 broadcast_in_dim.31
  140.7 0.0 copy-start.1
  140.7 36.5 %all_to_all.33 = bf16[4,3072,128]{2,1,0:T(8,128)(2,1)S(1)} all-to-all(bf16[4,3072,128]{2,1,0:T(8,128)(2,1)S(1)} %broadcast_in_dim.31), channel_id=1, replica_groups=mesh['y'=8,'core'=2,'x'=4,'z'=8] {'x'}, dimensions={0} | all-to-all | bytes 6291456 | tf_op jit(solution)/shard_map/all_to_all | solution.py:16
  177.2 0.0 copy-done.1
  177.2 4.2 %shard_map.47 = (f32[3072,128]{1,0:T(8,128)S(1)}, bf16[3072,128]{1,0:T(8,128)(2,1)S(1)}) custom-call(s32[1]{0:T(128)} %bitcast.refs_0_, s32[128]{0:T(128)S(1)} %bitcast.15, s32[128]{0:T(128)S(1)} %bitcast.17, bf16[128,128,128]{2,1,0:T(8,128)(2,1)S(1)} %bitcast.11, bf16[12288,128]{1,0:T(8,128)(2,1)S(1)} %bitcast.13), custom_call_target="tpu_custom_call" | custom-call | flops 536870912 | bytes 9699328 | tf_op jit(solution)/shard_map/pallas_call | solution.py:61
  181.4 6.7 %collective-permute-start.1 = (bf16[3072,128]{1,0:T(8,128)(2,1)S(1)}, bf16[3072,128]{1,0:T(8,128)(2,1)S(1)}, u32[]{:S(2)}, u32[]{:S(2)}) collective-permute-start(bf16[3072,128]{1,0:T(8,128)(2,1)S(1)} %get-tuple-element.12), channel_id=1, source_target_pairs={{0,32},{32,0},{1,33},{33,1},{2,34},{34,2},{3,35},{35,3},{4,36},{36... | collective-permute-start | bytes 2359304 | tf_op jit(solution)/shard_map/ppermute | solution.py:95
  188.1 1.9 collective-permute-done.1
  190.0 0.2 add_convert_fusion
  190.2 0.0 copy-start.4
  190.2 25.1 %all_to_all.34 = bf16[8,384,128]{2,1,0:T(8,128)(2,1)S(1)} all-to-all(bf16[8,384,128]{2,1,0:T(8,128)(2,1)S(1)} %bitcast.19), channel_id=1, replica_groups=mesh['y'=8,'core'=2,'x'=4,'z'=8] {'y'}, dimensions={0} | all-to-all | bytes 1572864 | tf_op jit(solution)/shard_map/all_to_all | solution.py:97
  215.3 0.1 reduce_sum.25
  215.4 0.0 copy-done.4
  215.4 0.7 add_convert_fusion.2
Async XLA Ops:
  35.3 39.0 %copy-start.2 = (s32[1,1,128]{2,1,0:T(1,128)S(1)}, s32[1,1,128]{2,1,0:T(1,128)}, u32[]{:S(2)}) copy-start(s32[1,1,128]{2,1,0:T(1,128)} %param.6) | copy-start | bytes 1540
  35.3 39.0 %copy-start.3 = (s32[1,1,128]{2,1,0:T(1,128)S(1)}, s32[1,1,128]{2,1,0:T(1,128)}, u32[]{:S(2)}) copy-start(s32[1,1,128]{2,1,0:T(1,128)} %param.7) | copy-start | bytes 1540
  35.3 39.0 %all-to-all-start.1 = ((bf16[4,3072,128]{2,1,0:T(8,128)(2,1)}), bf16[4,3072,128]{2,1,0:T(8,128)(2,1)S(1)}, u32[]{:S(2)}, u32[]{:S(2)}) async-start(bf16[4,3072,128]{2,1,0:T(8,128)(2,1)} %broadcast_in_dim.28), calls=%async_computation.1 | async-start | bytes 6291456 | tf_op jit(solution)/shard_map/all_to_all | solution.py:16
  74.3 2.2 %copy-start = (bf16[1,1,128,128,128]{4,3,2,1,0:T(8,128)(2,1)S(1)}, bf16[1,1,128,128,128]{4,3,2,1,0:T(8,128)(2,1)}, u32[]{:S(2)}) copy-start(bf16[1,1,128,128,128]{4,3,2,1,0:T(8,128)(2,1)} %param.5) | copy-start | bytes 12582916
  80.7 7.5 %collective-permute-start = (bf16[3072,128]{1,0:T(8,128)(2,1)S(1)}, bf16[3072,128]{1,0:T(8,128)(2,1)S(1)}, u32[]{:S(2)}, u32[]{:S(2)}) collective-permute-start(bf16[3072,128]{1,0:T(8,128)(2,1)S(1)} %get-tuple-element.10), channel_id=1, source_target_pairs={{0,32},{32,0},{1,33},{33,1},{2,34},{34,2},{3,35},{35,3},{4,36},{36... | collective-permute-start | bytes 2359304 | tf_op jit(solution)/shard_map/ppermute | solution.py:95
  140.7 36.5 %copy-start.1 = (bf16[1,1,128,128,128]{4,3,2,1,0:T(8,128)(2,1)S(1)}, bf16[1,1,128,128,128]{4,3,2,1,0:T(8,128)(2,1)}, u32[]{:S(2)}) copy-start(bf16[1,1,128,128,128]{4,3,2,1,0:T(8,128)(2,1)} %param.5) | copy-start | bytes 12582916
  181.4 8.6 %collective-permute-start.1 = (bf16[3072,128]{1,0:T(8,128)(2,1)S(1)}, bf16[3072,128]{1,0:T(8,128)(2,1)S(1)}, u32[]{:S(2)}, u32[]{:S(2)}) collective-permute-start(bf16[3072,128]{1,0:T(8,128)(2,1)S(1)} %get-tuple-element.12), channel_id=1, source_target_pairs={{0,32},{32,0},{1,33},{33,1},{2,34},{34,2},{3,35},{35,3},{4,36},{36... | collective-permute-start | bytes 2359304 | tf_op jit(solution)/shard_map/ppermute | solution.py:95
  190.2 25.2 %copy-start.4 = (bf16[384,128]{1,0:T(8,128)(2,1)S(1)}, bf16[384,128]{1,0:T(8,128)(2,1)}, u32[]{:S(2)}) copy-start(bf16[384,128]{1,0:T(8,128)(2,1)} %param.4) | copy-start | bytes 294916

commit v2 on v1

v2 whole, which is shorter than its diff:
```python
import jax
import jax.numpy as jnp
from jax import lax
from jax.experimental import pallas as pl
from jax.experimental.pallas import tpu as pltpu
from jax.sharding import Mesh
from jax.sharding import PartitionSpec as P

COL = ("x", "z")
ROW_COL = ("y", "core", "x", "z")
CHUNK = 16
EARLY = 96


def spread(piece, axis):
    copies = jnp.broadcast_to(piece[None], (lax.axis_size(axis), *piece.shape))
    return lax.all_to_all(copies, axis, split_axis=0, concat_axis=0, tiled=True)


def tile_kernel(slots_ref, tiles_hbm_ref, early_ref, late_ref, keep_ref, send_ref, tiles_ref, total_ref, sems):
    edge = tiles_ref.shape[-1]
    half = keep_ref.shape[0]

    def fetch(step):
        at = pl.ds(step * CHUNK, CHUNK)
        return pltpu.make_async_copy(tiles_hbm_ref.at[at], tiles_ref.at[at], sems.at[step])

    for step in range(sems.shape[0]):
        fetch(step).start()
    total_ref[...] = jnp.zeros_like(total_ref)

    @pl.loop(0, tiles_ref.shape[0] // CHUNK)
    def _(step):
        fetch(step).wait()
        products = []
        for k in range(CHUNK):
            slot = step * CHUNK + k
            is_early = slots_ref[1, slot] != 0
            early = early_ref[slots_ref[2, slot]]
            upper = late_ref[pl.ds(pl.multiple_of(slots_ref[3, slot], 32), EARLY), :]
            lower = late_ref[pl.ds(pl.multiple_of(slots_ref[4, slot], 32), edge - EARLY), :]
            block = jnp.concatenate([jnp.where(is_early, early, upper), lower], axis=0)
            products.append(jnp.dot(tiles_ref[slot], block, preferred_element_type=jnp.float32))
        for k, product in enumerate(products):
            total_ref[slots_ref[0, step * CHUNK + k]] += product

    keep_ref[...] = total_ref[:half].astype(keep_ref.dtype)
    send_ref[...] = total_ref[half : 2 * half].astype(send_ref.dtype)


def tile_products(slots, tiles, early, late, half):
    edge, columns = tiles.shape[-1], late.shape[-1]
    vmem = pl.BlockSpec(memory_space=pltpu.VMEM)
    return pl.pallas_call(
        tile_kernel,
        out_shape=[
            jax.ShapeDtypeStruct((half, edge, columns), jnp.float32),
            jax.ShapeDtypeStruct((half, edge, columns), jnp.bfloat16),
        ],
        in_specs=[pl.BlockSpec(memory_space=pltpu.SMEM), pl.BlockSpec(memory_space=pl.ANY), vmem, vmem],
        out_specs=[vmem, vmem],
        scratch_shapes=[
            pltpu.VMEM(tiles.shape, tiles.dtype),
            pltpu.VMEM((2 * half + 1, edge, columns), jnp.float32),
            pltpu.SemaphoreType.DMA((tiles.shape[0] // CHUNK,)),
        ],
        compiler_params=pltpu.CompilerParams(vmem_limit_bytes=24 << 20),
        cost_estimate=pl.CostEstimate(
            flops=2 * tiles.size * columns,
            bytes_accessed=2 * (tiles.size + early.size + late.size) + 6 * half * edge * columns,
            transcendentals=0,
        ),
    )(slots, pltpu.with_memory_space_constraint(tiles, pltpu.HBM), early.reshape(-1, EARLY, columns), late.reshape(-1, columns))


def body(demand, tile_data, tile_row, tile_col):
    tile_block = tile_data[0, 0]
    slot_rows = tile_row[0, 0]
    slot_cols = tile_col[0, 0]
    edge, columns = tile_block.shape[-1], demand.shape[1]
    chips, ring, line = lax.axis_size("y"), lax.axis_size("x"), lax.axis_size("z")
    span_tiles = demand.shape[0] // edge
    half = chips * span_tiles

    span = slot_rows // span_tiles
    other_core = lax.bitwise_xor(span % 2, lax.axis_index("core"))
    places = (span // 2) * span_tiles + slot_rows % span_tiles + half * other_core
    places = jnp.where(slot_rows >= 2 * half, 2 * half, places).astype(jnp.int32)

    device, tile = slot_cols // span_tiles, slot_cols % span_tiles
    late_rows = demand.shape[0] - EARLY
    lower_at = device * late_rows + tile * edge
    upper_at = jnp.where(tile == 0, lower_at, lower_at - EARLY)
    early_at = device % line * ring + device // line
    slots = jnp.stack([places, tile == 0, early_at, upper_at, lower_at]).astype(jnp.int32)

    def multiply(piece):
        early, late = piece[:EARLY], piece[EARLY:]
        late_line = spread(late, "z")
        early_line = lax.all_gather(early, "x")
        late_line, early_line = lax.optimization_barrier((late_line, early_line))
        late_panel = spread(late_line, "x")
        early_panel = lax.all_gather(early_line, "z")
        keep, send = tile_products(slots, tile_block, early_panel, late_panel, half)
        other = lax.ppermute(send, "core", [(0, 1), (1, 0)])
        both = (keep + other.astype(jnp.float32)).astype(jnp.bfloat16)
        arrived = lax.all_to_all(
            both.reshape(chips, -1, columns), "y", split_axis=0, concat_axis=0, tiled=True
        )
        return arrived.astype(jnp.float32).sum(axis=0).astype(jnp.bfloat16)

    first_term = multiply(demand)
    second_term = multiply(first_term)
    summed = (
        demand.astype(jnp.float32)
        + first_term.astype(jnp.float32)
        + second_term.astype(jnp.float32)
    )
    return summed.astype(jnp.bfloat16)


def solution(mesh):
    rows, cols = mesh.shape["row"], mesh.shape["col"]
    torus = Mesh(
        mesh.devices.reshape(rows // 2, 2, 4, cols // 4), ("y", "core", "x", "z")
    )
    return jax.shard_map(
        body,
        mesh=torus,
        in_specs=(
            P(ROW_COL, None),
            P(("y", "core"), COL, None, None, None),
            P(("y", "core"), COL, None),
            P(("y", "core"), COL, None),
        ),
        out_specs=P(ROW_COL, None),
        check_vma=False,
    )
```

time: 217 us -> 199 us (0.917)
  blocking collectives: 145 us -> 117 us
  starting transfers between devices: 16.4 us -> 30.7 us
  waiting for transfers between devices: 38.6 us -> 33.4 us
    all_to_all x3 -> x0, blocking collectives: 91.5 us -> none  [spread(): return lax.all_to_all(copies, axis, split_axis=0, concat_axis=0, tiled=True)]
    all_gather x0 -> x4, blocking collectives: none -> 62.6 us  [the longest x2 43.3 us: multiply(): early_panel = lax.all_gather(early_line, 'z')]
    all_to_all x1 -> x4, starting transfers between devices: 4.14 us -> 22.2 us  [spread(): return lax.all_to_all(copies, axis, split_axis=0, concat_axis=0, tiled=True)]
    all_to_all x1 -> x4, waiting for transfers between devices: 34.9 us -> 29.7 us  [spread(): return lax.all_to_all(copies, axis, split_axis=0, concat_axis=0, tiled=True)]
    ppermute x2, starting transfers between devices: 12.2 us -> 8.54 us  [multiply(): other = lax.ppermute(send, 'core', [(0, 1), (1, 0)])]
    unnamed x10 -> x6, local copies, waits for them, and re-layouts: 2.21 us -> 0.01 us
  transfers between devices with their start and end apart: 3 -> 6, of which waited for: 3 -> 6; matrix products, arithmetic and copies ran while one was open for 0% -> 0% of each run, Pallas kernels for 0% -> 0%
where the time goes in v2:
time: 199 us
  blocking collectives  117 us (59%)
  waiting for transfers between devices  33.4 us (17%)
  starting transfers between devices  30.7 us (15%)
  Pallas kernels  9.18 us (5%)
  local copies, waits for them, and re-layouts  6.26 us (3%)
    all_to_all x2, blocking collectives, multiply(): lax.all_to_all(both.reshape(chips, -1, columns), 'y', split_axis=0, conca...  54.8 us
    all_gather x2, blocking collectives, multiply(): early_panel = lax.all_gather(early_line, 'z')  43.3 us
    all_to_all x4, waiting for transfers between devices, spread(): return lax.all_to_all(copies, axis, split_axis=0, concat_axis=0, tiled=True)  29.7 us
    all_to_all x4, starting transfers between devices, spread(): return lax.all_to_all(copies, axis, split_axis=0, concat_axis=0, tiled=True)  22.2 us
    all_gather x2, blocking collectives, multiply(): early_line = lax.all_gather(early, 'x')  19.3 us
    pallas_call x2, Pallas kernels, tile_products(): pl.pallas_call(tile_kernel, out_shape=[jax.ShapeDtypeStruct((half, edge,...  9.18 us
    ppermute x2, starting transfers between devices, multiply(): other = lax.ppermute(send, 'core', [(0, 1), (1, 0)])  8.54 us
    broadcast_in_dim x4, local copies, waits for them, and re-layouts, spread(): copies = jnp.broadcast_to(piece[None], (lax.axis_size(axis), *piece.shape))  5.31 us
  transfers between devices with their start and end apart: 6, of which 6 were waited for; matrix products, arithmetic and copies ran while one was open for 0% of the time, Pallas kernels for 0%

profile of v2, /device:TPU:1, one launch (start us, length us, event | category | flops | bytes accessed | tf_op | source)
XLA Modules:
  0.0 198.6 jit_solution(10157522701593549553)
XLA Ops:
  0.0 0.0 slice-start
  0.0 0.9 slice.12
  0.9 0.9 broadcast_in_dim.10
  1.8 10.9 %all-to-all-start = ((bf16[8,288,128]{2,1,0:T(8,128)(2,1)}), bf16[8,288,128]{2,1,0:T(8,128)(2,1)S(1)}, u32[]{:S(2)}, u32[]{:S(2)}) async-start(bf16[8,288,128]{2,1,0:T(8,128)(2,1)} %broadcast_in_dim.10), calls=%async_computation | async-start | bytes 1179648 | tf_op jit(solution)/shard_map/all_to_all | solution.py:17
  12.7 0.0 slice-done
  12.7 10.0 %all-gather = bf16[384,128]{1,0:T(8,128)(2,1)S(1)} all-gather(bf16[96,128]{1,0:T(8,128)(2,1)S(1)} %slice-done), channel_id=2, replica_groups=mesh['y'=8,'core'=2,'x'=4,'z'=8] {'x'}, dimensions={0}, use_global_device_ids=true | all-gather | bytes 122880 | tf_op jit(solution)/shard_map/all_gather | solution.py:100
  22.6 9.4 %all-to-all-done = bf16[8,288,128]{2,1,0:T(8,128)(2,1)S(1)} async-done(((bf16[8,288,128]{2,1,0:T(8,128)(2,1)}), bf16[8,288,128]{2,1,0:T(8,128)(2,1)S(1)}, u32[]{:S(2)}, u32[]{:S(2)}) %all-to-all-start) | async-done | bytes 589856 | tf_op jit(solution)/shard_map/all_to_all | solution.py:17
  32.0 1.8 broadcast_in_dim.11
  33.8 0.0 copy-start.1
  33.8 0.0 copy-start.2
  33.8 4.1 %all-to-all-start.1 = ((bf16[4,8,288,128]{3,2,1,0:T(8,128)(2,1)}), bf16[4,8,288,128]{3,2,1,0:T(8,128)(2,1)S(1)}, u32[]{:S(2)}, u32[]{:S(2)}) async-start(bf16[4,8,288,128]{3,2,1,0:T(8,128)(2,1)} %broadcast_in_dim.11), calls=%async_computation.1 | async-start | bytes 4718592 | tf_op jit(solution)/shard_map/all_to_all | solution.py:17
  37.9 0.0 copy-done.1
  38.0 0.0 copy-done.2
  38.1 21.6 %all-gather.1.early_ref = bf16[32,96,128]{2,1,0:T(8,128)(2,1)S(1)} all-gather(bf16[4,96,128]{2,1,0:T(8,128)(2,1)S(1)} %bitcast.49), channel_id=3, replica_groups=mesh['y'=8,'core'=2,'x'=4,'z'=8] {'z'}, dimensions={0}, use_global_device_ids=true | all-gather | bytes 884736 | tf_op jit(solution)/shard_map/all_gather | solution.py:103
  59.6 6.7 %all-to-all-done.1 = bf16[4,8,288,128]{3,2,1,0:T(8,128)(2,1)S(1)} async-done(((bf16[4,8,288,128]{3,2,1,0:T(8,128)(2,1)}), bf16[4,8,288,128]{3,2,1,0:T(8,128)(2,1)S(1)}, u32[]{:S(2)}, u32[]{:S(2)}) %all-to-all-start.1) | async-done | bytes 2359328 | tf_op jit(solution)/shard_map/all_to_all | solution.py:17
  66.4 4.6 %shard_map.46 = (f32[24,128,128]{2,1,0:T(8,128)S(1)}, bf16[24,128,128]{2,1,0:T(8,128)(2,1)S(1)}) custom-call(s32[5,128]{1,0:T(8,128)S(1)} %stack.2.slots_ref, bf16[128,128,128]{2,1,0:T(8,128)(2,1)} %bitcast.45, bf16[32,96,128]{2,1,0:T(8,128)(2,1)S(1)} %all-gather.1.early_ref, bf16[9216,128]{1,0:T(8,128)(2,1)S(1)} %bitcast.43), custom_call_target="tpu_custom_call" | custom-call | flops 536870912 | bytes 9699328 | tf_op jit(solution)/shard_map/pallas_call | solution.py:54
  71.0 3.6 %collective-permute-start = (bf16[24,128,128]{2,1,0:T(8,128)(2,1)S(1)}, bf16[24,128,128]{2,1,0:T(8,128)(2,1)S(1)}, u32[]{:S(2)}, u32[]{:S(2)}) collective-permute-start(bf16[24,128,128]{2,1,0:T(8,128)(2,1)S(1)} %get-tuple-element.16), channel_id=1, source_target_pairs={{0,32},{32,0},{1,33},{33,1},{2,34},{34,2},{3,35},{35,3},{4,36},{36... | collective-permute-start | bytes 2359304 | tf_op jit(solution)/shard_map/ppermute | solution.py:105
  74.5 1.9 collective-permute-done
  76.4 0.2 add_convert_fusion.1
  76.7 29.0 %all_to_all.30 = bf16[8,384,128]{2,1,0:T(8,128)(2,1)S(1)} all-to-all(bf16[8,384,128]{2,1,0:T(8,128)(2,1)S(1)} %bitcast.47), channel_id=1, replica_groups=mesh['y'=8,'core'=2,'x'=4,'z'=8] {'y'}, dimensions={0} | all-to-all | bytes 1572864 | tf_op jit(solution)/shard_map/all_to_all | solution.py:107
  105.6 0.1 reduce_sum.24
  105.8 0.9 broadcast_in_dim.12
  106.7 3.5 %all-to-all-start.3 = ((bf16[8,288,128]{2,1,0:T(8,128)(2,1)}), bf16[8,288,128]{2,1,0:T(8,128)(2,1)S(1)}, u32[]{:S(2)}, u32[]{:S(2)}) async-start(bf16[8,288,128]{2,1,0:T(8,128)(2,1)} %broadcast_in_dim.12), calls=%async_computation.3 | async-start | bytes 1179648 | tf_op jit(solution)/shard_map/all_to_all | solution.py:17
  110.2 9.3 %all-gather.2 = bf16[384,128]{1,0:T(8,128)(2,1)S(1)} all-gather(bf16[96,128]{1,0:T(8,128)(2,1)S(1)} %slice.17), channel_id=4, replica_groups=mesh['y'=8,'core'=2,'x'=4,'z'=8] {'x'}, dimensions={0}, use_global_device_ids=true | all-gather | bytes 122880 | tf_op jit(solution)/shard_map/all_gather | solution.py:100
  119.5 8.3 %all-to-all-done.3 = bf16[8,288,128]{2,1,0:T(8,128)(2,1)S(1)} async-done(((bf16[8,288,128]{2,1,0:T(8,128)(2,1)}), bf16[8,288,128]{2,1,0:T(8,128)(2,1)S(1)}, u32[]{:S(2)}, u32[]{:S(2)}) %all-to-all-start.3) | async-done | bytes 589856 | tf_op jit(solution)/shard_map/all_to_all | solution.py:17
  127.8 1.8 broadcast_in_dim.13
  129.6 3.6 %all-to-all-start.4 = ((bf16[4,8,288,128]{3,2,1,0:T(8,128)(2,1)}), bf16[4,8,288,128]{3,2,1,0:T(8,128)(2,1)S(1)}, u32[]{:S(2)}, u32[]{:S(2)}) async-start(bf16[4,8,288,128]{3,2,1,0:T(8,128)(2,1)} %broadcast_in_dim.13), calls=%async_computation.4 | async-start | bytes 4718592 | tf_op jit(solution)/shard_map/all_to_all | solution.py:17
  133.2 21.7 %all-gather.3.early_ref = bf16[32,96,128]{2,1,0:T(8,128)(2,1)S(1)} all-gather(bf16[4,96,128]{2,1,0:T(8,128)(2,1)S(1)} %bitcast.50), channel_id=5, replica_groups=mesh['y'=8,'core'=2,'x'=4,'z'=8] {'z'}, dimensions={0}, use_global_device_ids=true | all-gather | bytes 884736 | tf_op jit(solution)/shard_map/all_gather | solution.py:103
  154.9 5.3 %all-to-all-done.4 = bf16[4,8,288,128]{3,2,1,0:T(8,128)(2,1)S(1)} async-done(((bf16[4,8,288,128]{3,2,1,0:T(8,128)(2,1)}), bf16[4,8,288,128]{3,2,1,0:T(8,128)(2,1)S(1)}, u32[]{:S(2)}, u32[]{:S(2)}) %all-to-all-start.4) | async-done | bytes 2359328 | tf_op jit(solution)/shard_map/all_to_all | solution.py:17
  160.2 4.6 %shard_map.47 = (f32[24,128,128]{2,1,0:T(8,128)S(1)}, bf16[24,128,128]{2,1,0:T(8,128)(2,1)S(1)}) custom-call(s32[5,128]{1,0:T(8,128)S(1)} %stack.2.slots_ref, bf16[128,128,128]{2,1,0:T(8,128)(2,1)} %bitcast.46, bf16[32,96,128]{2,1,0:T(8,128)(2,1)S(1)} %all-gather.3.early_ref, bf16[9216,128]{1,0:T(8,128)(2,1)S(1)} %bitcast.44), custom_call_target="tpu_custom_call" | custom-call | flops 536870912 | bytes 9699328 | tf_op jit(solution)/shard_map/pallas_call | solution.py:54
  164.8 5.0 %collective-permute-start.1 = (bf16[24,128,128]{2,1,0:T(8,128)(2,1)S(1)}, bf16[24,128,128]{2,1,0:T(8,128)(2,1)S(1)}, u32[]{:S(2)}, u32[]{:S(2)}) collective-permute-start(bf16[24,128,128]{2,1,0:T(8,128)(2,1)S(1)} %get-tuple-element.20), channel_id=1, source_target_pairs={{0,32},{32,0},{1,33},{33,1},{2,34},{34,2},{3,35},{35,3},{4,36},{36... | collective-permute-start | bytes 2359304 | tf_op jit(solution)/shard_map/ppermute | solution.py:105
  169.8 1.9 collective-permute-done.1
  171.7 0.2 add_convert_fusion
  171.9 0.0 copy-start
  171.9 25.9 %all_to_all.31 = bf16[8,384,128]{2,1,0:T(8,128)(2,1)S(1)} all-to-all(bf16[8,384,128]{2,1,0:T(8,128)(2,1)S(1)} %bitcast.48), channel_id=1, replica_groups=mesh['y'=8,'core'=2,'x'=4,'z'=8] {'y'}, dimensions={0} | all-to-all | bytes 1572864 | tf_op jit(solution)/shard_map/all_to_all | solution.py:107
  197.8 0.1 reduce_sum.25
  197.9 0.0 copy-done
  197.9 0.7 add_convert_fusion.2
  (7 shorter events, 0.1 us)
Async XLA Ops:
  0.0 12.7 %slice-start = ((bf16[384,128]{1,0:T(8,128)(2,1)}), bf16[96,128]{1,0:T(8,128)(2,1)S(1)}, s32[]{:S(2)}) async-start(bf16[384,128]{1,0:T(8,128)(2,1)} %param.4), calls=%async_computation.6 | async-start | bytes 49152 | tf_op jit(solution)/shard_map/slice | solution.py:98
  1.8 30.2 %all-to-all-start = ((bf16[8,288,128]{2,1,0:T(8,128)(2,1)}), bf16[8,288,128]{2,1,0:T(8,128)(2,1)S(1)}, u32[]{:S(2)}, u32[]{:S(2)}) async-start(bf16[8,288,128]{2,1,0:T(8,128)(2,1)} %broadcast_in_dim.10), calls=%async_computation | async-start | bytes 1179648 | tf_op jit(solution)/shard_map/all_to_all | solution.py:17
  33.8 4.2 %copy-start.1 = (s32[1,1,128]{2,1,0:T(1,128)S(1)}, s32[1,1,128]{2,1,0:T(1,128)}, u32[]{:S(2)}) copy-start(s32[1,1,128]{2,1,0:T(1,128)} %param.7) | copy-start | bytes 1540
  33.8 4.2 %copy-start.2 = (s32[1,1,128]{2,1,0:T(1,128)S(1)}, s32[1,1,128]{2,1,0:T(1,128)}, u32[]{:S(2)}) copy-start(s32[1,1,128]{2,1,0:T(1,128)} %param.6) | copy-start | bytes 1540
  33.8 32.6 %all-to-all-start.1 = ((bf16[4,8,288,128]{3,2,1,0:T(8,128)(2,1)}), bf16[4,8,288,128]{3,2,1,0:T(8,128)(2,1)S(1)}, u32[]{:S(2)}, u32[]{:S(2)}) async-start(bf16[4,8,288,128]{3,2,1,0:T(8,128)(2,1)} %broadcast_in_dim.11), calls=%async_computation.1 | async-start | bytes 4718592 | tf_op jit(solution)/shard_map/all_to_all | solution.py:17
  71.0 5.5 %collective-permute-start = (bf16[24,128,128]{2,1,0:T(8,128)(2,1)S(1)}, bf16[24,128,128]{2,1,0:T(8,128)(2,1)S(1)}, u32[]{:S(2)}, u32[]{:S(2)}) collective-permute-start(bf16[24,128,128]{2,1,0:T(8,128)(2,1)S(1)} %get-tuple-element.16), channel_id=1, source_target_pairs={{0,32},{32,0},{1,33},{33,1},{2,34},{34,2},{3,35},{35,3},{4,36},{36... | collective-permute-start | bytes 2359304 | tf_op jit(solution)/shard_map/ppermute | solution.py:105
  106.7 21.2 %all-to-all-start.3 = ((bf16[8,288,128]{2,1,0:T(8,128)(2,1)}), bf16[8,288,128]{2,1,0:T(8,128)(2,1)S(1)}, u32[]{:S(2)}, u32[]{:S(2)}) async-start(bf16[8,288,128]{2,1,0:T(8,128)(2,1)} %broadcast_in_dim.12), calls=%async_computation.3 | async-start | bytes 1179648 | tf_op jit(solution)/shard_map/all_to_all | solution.py:17
  129.6 30.6 %all-to-all-start.4 = ((bf16[4,8,288,128]{3,2,1,0:T(8,128)(2,1)}), bf16[4,8,288,128]{3,2,1,0:T(8,128)(2,1)S(1)}, u32[]{:S(2)}, u32[]{:S(2)}) async-start(bf16[4,8,288,128]{3,2,1,0:T(8,128)(2,1)} %broadcast_in_dim.13), calls=%async_computation.4 | async-start | bytes 4718592 | tf_op jit(solution)/shard_map/all_to_all | solution.py:17
  164.8 6.9 %collective-permute-start.1 = (bf16[24,128,128]{2,1,0:T(8,128)(2,1)S(1)}, bf16[24,128,128]{2,1,0:T(8,128)(2,1)S(1)}, u32[]{:S(2)}, u32[]{:S(2)}) collective-permute-start(bf16[24,128,128]{2,1,0:T(8,128)(2,1)S(1)} %get-tuple-element.20), channel_id=1, source_target_pairs={{0,32},{32,0},{1,33},{33,1},{2,34},{34,2},{3,35},{35,3},{4,36},{36... | collective-permute-start | bytes 2359304 | tf_op jit(solution)/shard_map/ppermute | solution.py:105
  171.9 26.0 %copy-start = (bf16[384,128]{1,0:T(8,128)(2,1)S(1)}, bf16[384,128]{1,0:T(8,128)(2,1)}, u32[]{:S(2)}) copy-start(bf16[384,128]{1,0:T(8,128)(2,1)} %param.4) | copy-start | bytes 294916

commit v3 on v2

--- a/solution.py
+++ b/solution.py
@@ -6,10 +6,11 @@
 from jax.sharding import Mesh
 from jax.sharding import PartitionSpec as P
 
-COL = ("x", "z")
-ROW_COL = ("y", "core", "x", "z")
+Z = ("z_pair", "z_end")
+COL = ("x", *Z)
+ROW_COL = ("y", "core", *COL)
 CHUNK = 16
-EARLY = 96
+EARLY = 112
 
 
 def spread(piece, axis):
@@ -37,8 +38,8 @@
             slot = step * CHUNK + k
             is_early = slots_ref[1, slot] != 0
             early = early_ref[slots_ref[2, slot]]
-            upper = late_ref[pl.ds(pl.multiple_of(slots_ref[3, slot], 32), EARLY), :]
-            lower = late_ref[pl.ds(pl.multiple_of(slots_ref[4, slot], 32), edge - EARLY), :]
+            upper = late_ref[pl.ds(pl.multiple_of(slots_ref[3, slot], 16), EARLY), :]
+            lower = late_ref[pl.ds(pl.multiple_of(slots_ref[4, slot], 16), edge - EARLY), :]
             block = jnp.concatenate([jnp.where(is_early, early, upper), lower], axis=0)
             products.append(jnp.dot(tiles_ref[slot], block, preferred_element_type=jnp.float32))
         for k, product in enumerate(products):
@@ -78,7 +79,7 @@
     slot_rows = tile_row[0, 0]
     slot_cols = tile_col[0, 0]
     edge, columns = tile_block.shape[-1], demand.shape[1]
-    chips, ring, line = lax.axis_size("y"), lax.axis_size("x"), lax.axis_size("z")
+    chips, ring, line = lax.axis_size("y"), lax.axis_size("x"), lax.axis_size(Z)
     span_tiles = demand.shape[0] // edge
     half = chips * span_tiles
 
@@ -96,11 +97,11 @@
 
     def multiply(piece):
         early, late = piece[:EARLY], piece[EARLY:]
-        late_line = spread(late, "z")
+        late_line = spread(late, Z)
         early_line = lax.all_gather(early, "x")
         late_line, early_line = lax.optimization_barrier((late_line, early_line))
         late_panel = spread(late_line, "x")
-        early_panel = lax.all_gather(early_line, "z")
+        early_panel = lax.all_gather(lax.all_gather(early_line, "z_end"), "z_pair")
         keep, send = tile_products(slots, tile_block, early_panel, late_panel, half)
         other = lax.ppermute(send, "core", [(0, 1), (1, 0)])
         both = (keep + other.astype(jnp.float32)).astype(jnp.bfloat16)
@@ -122,7 +123,7 @@
 def solution(mesh):
     rows, cols = mesh.shape["row"], mesh.shape["col"]
     torus = Mesh(
-        mesh.devices.reshape(rows // 2, 2, 4, cols // 4), ("y", "core", "x", "z")
+        mesh.devices.reshape(rows // 2, 2, 4, cols // 8, 2), ROW_COL
     )
     return jax.shard_map(
         body,

time: 199 us -> 195 us (0.980)
  waiting for transfers between devices: 33.4 us -> 27 us
  blocking collectives: 117 us -> 119 us
    all_to_all x4, waiting for transfers between devices: 29.7 us -> 23.3 us  [spread(): return lax.all_to_all(copies, axis, split_axis=0, concat_axis=0, tiled=True)]
    all_gather x2 -> x4, blocking collectives: 43.3 us -> 44.3 us  [multiply(): early_panel = lax.all_gather(lax.all_gather(early_line, 'z_end'), 'z_pair')]
where the time goes in v3:
time: 195 us; the launch traced here: 194 us
  blocking collectives  119 us (61%)
  starting transfers between devices  31.1 us (16%)
  waiting for transfers between devices  27 us (14%)
  Pallas kernels  9.24 us (5%)
  local copies, waits for them, and re-layouts  6 us (3%)
    all_to_all x2, blocking collectives, multiply(): lax.all_to_all(both.reshape(chips, -1, columns), 'y', split_axis=0, conca...  55.2 us
    all_gather x4, blocking collectives, multiply(): early_panel = lax.all_gather(lax.all_gather(early_line, 'z_end'), 'z_pair')  44.3 us
    all_to_all x4, waiting for transfers between devices, spread(): return lax.all_to_all(copies, axis, split_axis=0, concat_axis=0, tiled=True)  23.3 us
    all_to_all x4, starting transfers between devices, spread(): return lax.all_to_all(copies, axis, split_axis=0, concat_axis=0, tiled=True)  22.2 us
    all_gather x2, blocking collectives, multiply(): early_line = lax.all_gather(early, 'x')  19.8 us
    pallas_call x2, Pallas kernels, tile_products(): pl.pallas_call(tile_kernel, out_shape=[jax.ShapeDtypeStruct((half, edge,...  9.24 us
    ppermute x2, starting transfers between devices, multiply(): other = lax.ppermute(send, 'core', [(0, 1), (1, 0)])  8.89 us
    broadcast_in_dim x4, local copies, waits for them, and re-layouts, spread(): copies = jnp.broadcast_to(piece[None], (lax.axis_size(axis), *piece.shape))  5.05 us
  transfers between devices with their start and end apart: 6, of which 6 were waited for; matrix products, arithmetic and copies ran while one was open for 0% of the time, Pallas kernels for 0%

profile of v3, /device:TPU:1, one launch (start us, length us, event | category | flops | bytes accessed | tf_op | source)
XLA Modules:
  0.0 194.2 jit_solution(3337657867598353281)
XLA Ops:
  0.0 0.0 slice-start
  0.0 0.9 slice.12
  0.9 0.9 broadcast_in_dim.10
  1.8 10.9 %all-to-all-start = ((bf16[8,272,128]{2,1,0:T(8,128)(2,1)}), bf16[8,272,128]{2,1,0:T(8,128)(2,1)S(1)}, u32[]{:S(2)}, u32[]{:S(2)}) async-start(bf16[8,272,128]{2,1,0:T(8,128)(2,1)} %broadcast_in_dim.10), calls=%async_computation | async-start | bytes 1114112 | tf_op jit(solution)/shard_map/all_to_all | solution.py:18
  12.6 0.0 slice-done
  12.6 10.0 %all-gather = bf16[448,128]{1,0:T(8,128)(2,1)S(1)} all-gather(bf16[112,128]{1,0:T(8,128)(2,1)S(1)} %slice-done), channel_id=2, replica_groups=mesh['y'=8,'core'=2,'x'=4,'z_pair'=4,'z_end'=2] {'x'}, dimensions={0}, use_global_device_ids=true | all-gather | bytes 143360 | tf_op jit(solution)/shard_map/all_gather | solution.py:101
  22.7 8.6 %all-to-all-done = bf16[8,272,128]{2,1,0:T(8,128)(2,1)S(1)} async-done(((bf16[8,272,128]{2,1,0:T(8,128)(2,1)}), bf16[8,272,128]{2,1,0:T(8,128)(2,1)S(1)}, u32[]{:S(2)}, u32[]{:S(2)}) %all-to-all-start) | async-done | bytes 557088 | tf_op jit(solution)/shard_map/all_to_all | solution.py:18
  31.3 1.7 broadcast_in_dim.11
  33.0 0.0 copy-start.1
  33.0 0.0 copy-start.2
  33.0 4.1 %all-to-all-start.1 = ((bf16[4,8,272,128]{3,2,1,0:T(8,128)(2,1)}), bf16[4,8,272,128]{3,2,1,0:T(8,128)(2,1)S(1)}, u32[]{:S(2)}, u32[]{:S(2)}) async-start(bf16[4,8,272,128]{3,2,1,0:T(8,128)(2,1)} %broadcast_in_dim.11), calls=%async_computation.1 | async-start | bytes 4456448 | tf_op jit(solution)/shard_map/all_to_all | solution.py:18
  37.1 0.0 copy-done.1
  37.1 0.0 copy-done.2
  37.2 4.6 %all-gather.1 = bf16[8,112,128]{2,1,0:T(8,128)(2,1)S(1)} all-gather(bf16[4,112,128]{2,1,0:T(8,128)(2,1)S(1)} %bitcast.57), channel_id=3, replica_groups=mesh['y'=8,'core'=2,'x'=4,'z_pair'=4,'z_end'=2] {'z_end'}, dimensions={0}, use_global_device_ids=true | all-gather | bytes 344064 | tf_op jit(solution)/shard_map/all_gather | solution.py:104
  41.8 17.1 %all-gather.2 = bf16[8,4,112,128]{3,2,1,0:T(8,128)(2,1)S(1)} all-gather(bf16[2,4,112,128]{3,2,1,0:T(8,128)(2,1)S(1)} %bitcast.55), channel_id=4, replica_groups=mesh['y'=8,'core'=2,'x'=4,'z_pair'=4,'z_end'=2] {'z_pair'}, dimensions={0}, use_global_device_ids=true | all-gather | bytes 1146880 | tf_op jit(solution)/shard_map/all_gather | solution.py:104
  58.9 5.2 %all-to-all-done.1 = bf16[4,8,272,128]{3,2,1,0:T(8,128)(2,1)S(1)} async-done(((bf16[4,8,272,128]{3,2,1,0:T(8,128)(2,1)}), bf16[4,8,272,128]{3,2,1,0:T(8,128)(2,1)S(1)}, u32[]{:S(2)}, u32[]{:S(2)}) %all-to-all-start.1) | async-done | bytes 2228256 | tf_op jit(solution)/shard_map/all_to_all | solution.py:18
  64.1 4.6 %shard_map.46 = (f32[24,128,128]{2,1,0:T(8,128)S(1)}, bf16[24,128,128]{2,1,0:T(8,128)(2,1)S(1)}) custom-call(s32[5,128]{1,0:T(8,128)S(1)} %stack.2.slots_ref, bf16[128,128,128]{2,1,0:T(8,128)(2,1)} %bitcast.51, bf16[32,112,128]{2,1,0:T(8,128)(2,1)S(1)} %bitcast.50, bf16[8704,128]{1,0:T(8,128)(2,1)S(1)} %bitcast.47), custom_call_target="tpu_custom_call" | custom-call | flops 536870912 | bytes 9699328 | tf_op jit(solution)/shard_map/pallas_call | solution.py:55
  68.8 3.5 %collective-permute-start = (bf16[24,128,128]{2,1,0:T(8,128)(2,1)S(1)}, bf16[24,128,128]{2,1,0:T(8,128)(2,1)S(1)}, u32[]{:S(2)}, u32[]{:S(2)}) collective-permute-start(bf16[24,128,128]{2,1,0:T(8,128)(2,1)S(1)} %get-tuple-element.16), channel_id=1, source_target_pairs={{0,32},{32,0},{1,33},{33,1},{2,34},{34,2},{3,35},{35,3},{4,36},{36... | collective-permute-start | bytes 2359304 | tf_op jit(solution)/shard_map/ppermute | solution.py:106
  72.3 1.9 collective-permute-done
  74.2 0.2 add_convert_fusion.1
  74.4 29.0 %all_to_all.30 = bf16[8,384,128]{2,1,0:T(8,128)(2,1)S(1)} all-to-all(bf16[8,384,128]{2,1,0:T(8,128)(2,1)S(1)} %bitcast.53), channel_id=1, replica_groups=mesh['y'=8,'core'=2,'x'=4,'z_pair'=4,'z_end'=2] {'y'}, dimensions={0} | all-to-all | bytes 1572864 | tf_op jit(solution)/shard_map/all_to_all | solution.py:108
  103.4 0.1 reduce_sum.24
  103.5 0.9 broadcast_in_dim.12
  104.4 3.5 %all-to-all-start.3 = ((bf16[8,272,128]{2,1,0:T(8,128)(2,1)}), bf16[8,272,128]{2,1,0:T(8,128)(2,1)S(1)}, u32[]{:S(2)}, u32[]{:S(2)}) async-start(bf16[8,272,128]{2,1,0:T(8,128)(2,1)} %broadcast_in_dim.12), calls=%async_computation.3 | async-start | bytes 1114112 | tf_op jit(solution)/shard_map/all_to_all | solution.py:18
  108.0 9.8 %all-gather.3 = bf16[448,128]{1,0:T(8,128)(2,1)S(1)} all-gather(bf16[112,128]{1,0:T(8,128)(2,1)S(1)} %slice.17), channel_id=5, replica_groups=mesh['y'=8,'core'=2,'x'=4,'z_pair'=4,'z_end'=2] {'x'}, dimensions={0}, use_global_device_ids=true | all-gather | bytes 143360 | tf_op jit(solution)/shard_map/all_gather | solution.py:101
  117.7 6.8 %all-to-all-done.3 = bf16[8,272,128]{2,1,0:T(8,128)(2,1)S(1)} async-done(((bf16[8,272,128]{2,1,0:T(8,128)(2,1)}), bf16[8,272,128]{2,1,0:T(8,128)(2,1)S(1)}, u32[]{:S(2)}, u32[]{:S(2)}) %all-to-all-start.3) | async-done | bytes 557088 | tf_op jit(solution)/shard_map/all_to_all | solution.py:18
  124.5 1.7 broadcast_in_dim.13
  126.2 3.6 %all-to-all-start.4 = ((bf16[4,8,272,128]{3,2,1,0:T(8,128)(2,1)}), bf16[4,8,272,128]{3,2,1,0:T(8,128)(2,1)S(1)}, u32[]{:S(2)}, u32[]{:S(2)}) async-start(bf16[4,8,272,128]{3,2,1,0:T(8,128)(2,1)} %broadcast_in_dim.13), calls=%async_computation.4 | async-start | bytes 4456448 | tf_op jit(solution)/shard_map/all_to_all | solution.py:18
  129.8 4.3 %all-gather.4 = bf16[8,112,128]{2,1,0:T(8,128)(2,1)S(1)} all-gather(bf16[4,112,128]{2,1,0:T(8,128)(2,1)S(1)} %bitcast.58), channel_id=6, replica_groups=mesh['y'=8,'core'=2,'x'=4,'z_pair'=4,'z_end'=2] {'z_end'}, dimensions={0}, use_global_device_ids=true | all-gather | bytes 344064 | tf_op jit(solution)/shard_map/all_gather | solution.py:104
  134.1 18.3 %all-gather.5 = bf16[8,4,112,128]{3,2,1,0:T(8,128)(2,1)S(1)} all-gather(bf16[2,4,112,128]{3,2,1,0:T(8,128)(2,1)S(1)} %bitcast.56), channel_id=7, replica_groups=mesh['y'=8,'core'=2,'x'=4,'z_pair'=4,'z_end'=2] {'z_pair'}, dimensions={0}, use_global_device_ids=true | all-gather | bytes 1146880 | tf_op jit(solution)/shard_map/all_gather | solution.py:104
  152.4 2.6 %all-to-all-done.4 = bf16[4,8,272,128]{3,2,1,0:T(8,128)(2,1)S(1)} async-done(((bf16[4,8,272,128]{3,2,1,0:T(8,128)(2,1)}), bf16[4,8,272,128]{3,2,1,0:T(8,128)(2,1)S(1)}, u32[]{:S(2)}, u32[]{:S(2)}) %all-to-all-start.4) | async-done | bytes 2228256 | tf_op jit(solution)/shard_map/all_to_all | solution.py:18
  155.1 4.6 %shard_map.47 = (f32[24,128,128]{2,1,0:T(8,128)S(1)}, bf16[24,128,128]{2,1,0:T(8,128)(2,1)S(1)}) custom-call(s32[5,128]{1,0:T(8,128)S(1)} %stack.2.slots_ref, bf16[128,128,128]{2,1,0:T(8,128)(2,1)} %bitcast.52, bf16[32,112,128]{2,1,0:T(8,128)(2,1)S(1)} %bitcast.49, bf16[8704,128]{1,0:T(8,128)(2,1)S(1)} %bitcast.48), custom_call_target="tpu_custom_call" | custom-call | flops 536870912 | bytes 9699328 | tf_op jit(solution)/shard_map/pallas_call | solution.py:55
  159.7 5.3 %collective-permute-start.1 = (bf16[24,128,128]{2,1,0:T(8,128)(2,1)S(1)}, bf16[24,128,128]{2,1,0:T(8,128)(2,1)S(1)}, u32[]{:S(2)}, u32[]{:S(2)}) collective-permute-start(bf16[24,128,128]{2,1,0:T(8,128)(2,1)S(1)} %get-tuple-element.20), channel_id=1, source_target_pairs={{0,32},{32,0},{1,33},{33,1},{2,34},{34,2},{3,35},{35,3},{4,36},{36... | collective-permute-start | bytes 2359304 | tf_op jit(solution)/shard_map/ppermute | solution.py:106
  165.0 1.9 collective-permute-done.1
  166.9 0.2 add_convert_fusion
  167.2 0.0 copy-start
  167.2 26.2 %all_to_all.31 = bf16[8,384,128]{2,1,0:T(8,128)(2,1)S(1)} all-to-all(bf16[8,384,128]{2,1,0:T(8,128)(2,1)S(1)} %bitcast.54), channel_id=1, replica_groups=mesh['y'=8,'core'=2,'x'=4,'z_pair'=4,'z_end'=2] {'y'}, dimensions={0} | all-to-all | bytes 1572864 | tf_op jit(solution)/shard_map/all_to_all | solution.py:108
  193.4 0.1 reduce_sum.25
  193.5 0.0 copy-done
  193.5 0.7 add_convert_fusion.2
  (7 shorter events, 0.1 us)
Async XLA Ops:
  0.0 12.6 %slice-start = ((bf16[384,128]{1,0:T(8,128)(2,1)}), bf16[112,128]{1,0:T(8,128)(2,1)S(1)}, s32[]{:S(2)}) async-start(bf16[384,128]{1,0:T(8,128)(2,1)} %param.4), calls=%async_computation.6 | async-start | bytes 57344 | tf_op jit(solution)/shard_map/slice | solution.py:99
  1.8 29.5 %all-to-all-start = ((bf16[8,272,128]{2,1,0:T(8,128)(2,1)}), bf16[8,272,128]{2,1,0:T(8,128)(2,1)S(1)}, u32[]{:S(2)}, u32[]{:S(2)}) async-start(bf16[8,272,128]{2,1,0:T(8,128)(2,1)} %broadcast_in_dim.10), calls=%async_computation | async-start | bytes 1114112 | tf_op jit(solution)/shard_map/all_to_all | solution.py:18
  33.0 4.2 %copy-start.1 = (s32[1,1,128]{2,1,0:T(1,128)S(1)}, s32[1,1,128]{2,1,0:T(1,128)}, u32[]{:S(2)}) copy-start(s32[1,1,128]{2,1,0:T(1,128)} %param.7) | copy-start | bytes 1540
  33.0 4.2 %copy-start.2 = (s32[1,1,128]{2,1,0:T(1,128)S(1)}, s32[1,1,128]{2,1,0:T(1,128)}, u32[]{:S(2)}) copy-start(s32[1,1,128]{2,1,0:T(1,128)} %param.6) | copy-start | bytes 1540
  33.0 31.2 %all-to-all-start.1 = ((bf16[4,8,272,128]{3,2,1,0:T(8,128)(2,1)}), bf16[4,8,272,128]{3,2,1,0:T(8,128)(2,1)S(1)}, u32[]{:S(2)}, u32[]{:S(2)}) async-start(bf16[4,8,272,128]{3,2,1,0:T(8,128)(2,1)} %broadcast_in_dim.11), calls=%async_computation.1 | async-start | bytes 4456448 | tf_op jit(solution)/shard_map/all_to_all | solution.py:18
  68.8 5.4 %collective-permute-start = (bf16[24,128,128]{2,1,0:T(8,128)(2,1)S(1)}, bf16[24,128,128]{2,1,0:T(8,128)(2,1)S(1)}, u32[]{:S(2)}, u32[]{:S(2)}) collective-permute-start(bf16[24,128,128]{2,1,0:T(8,128)(2,1)S(1)} %get-tuple-element.16), channel_id=1, source_target_pairs={{0,32},{32,0},{1,33},{33,1},{2,34},{34,2},{3,35},{35,3},{4,36},{36... | collective-permute-start | bytes 2359304 | tf_op jit(solution)/shard_map/ppermute | solution.py:106
  104.4 20.1 %all-to-all-start.3 = ((bf16[8,272,128]{2,1,0:T(8,128)(2,1)}), bf16[8,272,128]{2,1,0:T(8,128)(2,1)S(1)}, u32[]{:S(2)}, u32[]{:S(2)}) async-start(bf16[8,272,128]{2,1,0:T(8,128)(2,1)} %broadcast_in_dim.12), calls=%async_computation.3 | async-start | bytes 1114112 | tf_op jit(solution)/shard_map/all_to_all | solution.py:18
  126.2 28.9 %all-to-all-start.4 = ((bf16[4,8,272,128]{3,2,1,0:T(8,128)(2,1)}), bf16[4,8,272,128]{3,2,1,0:T(8,128)(2,1)S(1)}, u32[]{:S(2)}, u32[]{:S(2)}) async-start(bf16[4,8,272,128]{3,2,1,0:T(8,128)(2,1)} %broadcast_in_dim.13), calls=%async_computation.4 | async-start | bytes 4456448 | tf_op jit(solution)/shard_map/all_to_all | solution.py:18
  159.7 7.2 %collective-permute-start.1 = (bf16[24,128,128]{2,1,0:T(8,128)(2,1)S(1)}, bf16[24,128,128]{2,1,0:T(8,128)(2,1)S(1)}, u32[]{:S(2)}, u32[]{:S(2)}) collective-permute-start(bf16[24,128,128]{2,1,0:T(8,128)(2,1)S(1)} %get-tuple-element.20), channel_id=1, source_target_pairs={{0,32},{32,0},{1,33},{33,1},{2,34},{34,2},{3,35},{35,3},{4,36},{36... | collective-permute-start | bytes 2359304 | tf_op jit(solution)/shard_map/ppermute | solution.py:106
  167.2 26.3 %copy-start = (bf16[384,128]{1,0:T(8,128)(2,1)S(1)}, bf16[384,128]{1,0:T(8,128)(2,1)}, u32[]{:S(2)}) copy-start(bf16[384,128]{1,0:T(8,128)(2,1)} %param.4) | copy-start | bytes 294916

commit v4 on v3

--- a/solution.py
+++ b/solution.py
@@ -18,13 +18,16 @@
     return lax.all_to_all(copies, axis, split_axis=0, concat_axis=0, tiled=True)
 
 
-def tile_kernel(slots_ref, tiles_hbm_ref, early_ref, late_ref, keep_ref, send_ref, tiles_ref, total_ref, sems):
+def tile_kernel(slots_ref, tiles_hbm_ref, row_ref, early_ref, late_ref, keep_ref, send_ref, tiles_ref, total_ref, sems):
     edge = tiles_ref.shape[-1]
     half = keep_ref.shape[0]
 
     def fetch(step):
         at = pl.ds(step * CHUNK, CHUNK)
         return pltpu.make_async_copy(tiles_hbm_ref.at[at], tiles_ref.at[at], sems.at[step])
+
+    def rows(ref, start, size):
+        return ref[pl.ds(pl.multiple_of(start, 16), size), :]
 
     for step in range(sems.shape[0]):
         fetch(step).start()
@@ -36,11 +39,11 @@
         products = []
         for k in range(CHUNK):
             slot = step * CHUNK + k
-            is_early = slots_ref[1, slot] != 0
-            early = early_ref[slots_ref[2, slot]]
-            upper = late_ref[pl.ds(pl.multiple_of(slots_ref[3, slot], 16), EARLY), :]
-            lower = late_ref[pl.ds(pl.multiple_of(slots_ref[4, slot], 16), edge - EARLY), :]
-            block = jnp.concatenate([jnp.where(is_early, early, upper), lower], axis=0)
+            early = early_ref[slots_ref[3, slot]]
+            upper = rows(late_ref, slots_ref[4, slot], EARLY)
+            lower = rows(late_ref, slots_ref[5, slot], edge - EARLY)
+            block = jnp.concatenate([jnp.where(slots_ref[2, slot] != 0, early, upper), lower], axis=0)
+            block = jnp.where(slots_ref[1, slot] != 0, rows(row_ref, slots_ref[6, slot], edge), block)
             products.append(jnp.dot(tiles_ref[slot], block, preferred_element_type=jnp.float32))
         for k, product in enumerate(products):
             total_ref[slots_ref[0, step * CHUNK + k]] += product
@@ -49,7 +52,7 @@
     send_ref[...] = total_ref[half : 2 * half].astype(send_ref.dtype)
 
 
-def tile_products(slots, tiles, early, late, half):
+def tile_products(slots, tiles, row, early, late, half):
     edge, columns = tiles.shape[-1], late.shape[-1]
     vmem = pl.BlockSpec(memory_space=pltpu.VMEM)
     return pl.pallas_call(
@@ -58,7 +61,7 @@
             jax.ShapeDtypeStruct((half, edge, columns), jnp.float32),
             jax.ShapeDtypeStruct((half, edge, columns), jnp.bfloat16),
         ],
-        in_specs=[pl.BlockSpec(memory_space=pltpu.SMEM), pl.BlockSpec(memory_space=pl.ANY), vmem, vmem],
+        in_specs=[pl.BlockSpec(memory_space=pltpu.SMEM), pl.BlockSpec(memory_space=pl.ANY), vmem, vmem, vmem],
         out_specs=[vmem, vmem],
         scratch_shapes=[
             pltpu.VMEM(tiles.shape, tiles.dtype),
@@ -71,7 +74,7 @@
             bytes_accessed=2 * (tiles.size + early.size + late.size) + 6 * half * edge * columns,
             transcendentals=0,
         ),
-    )(slots, pltpu.with_memory_space_constraint(tiles, pltpu.HBM), early.reshape(-1, EARLY, columns), late.reshape(-1, columns))
+    )(slots, pltpu.with_memory_space_constraint(tiles, pltpu.HBM), row.reshape(-1, columns), early.reshape(-1, EARLY, columns), late.reshape(-1, columns))
 
 
 def body(demand, tile_data, tile_row, tile_col):
@@ -89,20 +92,25 @@
     places = jnp.where(slot_rows >= 2 * half, 2 * half, places).astype(jnp.int32)
 
     device, tile = slot_cols // span_tiles, slot_cols % span_tiles
+    at_x, at_z, my_z = device // line, device % line, lax.axis_index(Z)
     late_rows = demand.shape[0] - EARLY
-    lower_at = device * late_rows + tile * edge
+    own = at_z == my_z
+    sent_at = jnp.where(own, 0, jnp.where(at_z == line - 1, my_z, at_z))
+    lower_at = (at_x * (line - 1) + sent_at) * late_rows + tile * edge
     upper_at = jnp.where(tile == 0, lower_at, lower_at - EARLY)
-    early_at = device % line * ring + device // line
-    slots = jnp.stack([places, tile == 0, early_at, upper_at, lower_at]).astype(jnp.int32)
+    early_at = at_z * ring + at_x
+    row_at = at_x * demand.shape[0] + tile * edge
+    slots = jnp.stack([places, own, tile == 0, early_at, upper_at, lower_at, row_at]).astype(jnp.int32)
 
     def multiply(piece):
-        early, late = piece[:EARLY], piece[EARLY:]
-        late_line = spread(late, Z)
-        early_line = lax.all_gather(early, "x")
-        late_line, early_line = lax.optimization_barrier((late_line, early_line))
-        late_panel = spread(late_line, "x")
-        early_panel = lax.all_gather(lax.all_gather(early_line, "z_end"), "z_pair")
-        keep, send = tile_products(slots, tile_block, early_panel, late_panel, half)
+        late_line = spread(piece[EARLY:], Z)
+        row = lax.all_gather(piece, "x")
+        early_pair = lax.all_gather(row[:, :EARLY], "z_end")
+        late_line, early_pair = lax.optimization_barrier((late_line, early_pair))
+        others = lax.dynamic_update_index_in_dim(late_line, late_line[-1], my_z, 0)[:-1]
+        late_panel = spread(others, "x")
+        early_panel = lax.all_gather(early_pair, "z_pair")
+        keep, send = tile_products(slots, tile_block, row, early_panel, late_panel, half)
         other = lax.ppermute(send, "core", [(0, 1), (1, 0)])
         both = (keep + other.astype(jnp.float32)).astype(jnp.bfloat16)
         arrived = lax.all_to_all(

time: 195 us -> 189 us (0.969)
  waiting for transfers between devices: 27 us -> 15.8 us
  blocking collectives: 119 us -> 122 us
    all_to_all x4, waiting for transfers between devices: 23.3 us -> 12 us  [spread(): return lax.all_to_all(copies, axis, split_axis=0, concat_axis=0, tiled=True)]
    all_gather x6, blocking collectives: 64.1 us -> 67.9 us  [the longest x2 36.4 us: multiply(): early_panel = lax.all_gather(early_pair, 'z_pair')]
where the time goes in v4:
time: 189 us; the launch traced here: 188 us
  blocking collectives  122 us (65%)
  starting transfers between devices  32.3 us (17%)
  waiting for transfers between devices  15.8 us (8%)
  Pallas kernels  10 us (5%)
  local copies, waits for them, and re-layouts  5.98 us (3%)
    all_to_all x2, blocking collectives, multiply(): lax.all_to_all(both.reshape(chips, -1, columns), 'y', split_axis=0, conca...  54.3 us
    all_gather x2, blocking collectives, multiply(): early_panel = lax.all_gather(early_pair, 'z_pair')  36.4 us
    all_to_all x4, starting transfers between devices, spread(): return lax.all_to_all(copies, axis, split_axis=0, concat_axis=0, tiled=True)  22.1 us
    all_gather x2, blocking collectives, multiply(): row = lax.all_gather(piece, 'x')  21.7 us
    all_to_all x4, waiting for transfers between devices, spread(): return lax.all_to_all(copies, axis, split_axis=0, concat_axis=0, tiled=True)  12 us
    ppermute x2, starting transfers between devices, multiply(): other = lax.ppermute(send, 'core', [(0, 1), (1, 0)])  10.2 us
    pallas_call x2, Pallas kernels, tile_products(): pl.pallas_call(tile_kernel, out_shape=[jax.ShapeDtypeStruct((half, edge,...  10 us
    all_gather x2, blocking collectives, multiply(): early_pair = lax.all_gather(row[:, :EARLY], 'z_end')  9.89 us
  transfers between devices with their start and end apart: 6, of which 6 were waited for; matrix products, arithmetic and copies ran while one was open for 0% of the time, Pallas kernels for 0%

profile of v4, /device:TPU:1, one launch (start us, length us, event | category | flops | bytes accessed | tf_op | source)
XLA Modules:
  0.0 188.1 jit_solution(4584955300729370155)
XLA Ops:
  0.0 0.0 copy-start
  0.0 1.0 slice.24
  1.0 0.9 broadcast_in_dim.16
  1.8 10.9 %all-to-all-start = ((bf16[8,272,128]{2,1,0:T(8,128)(2,1)}), bf16[8,272,128]{2,1,0:T(8,128)(2,1)S(1)}, u32[]{:S(2)}, u32[]{:S(2)}) async-start(bf16[8,272,128]{2,1,0:T(8,128)(2,1)} %broadcast_in_dim.16), calls=%async_computation | async-start | bytes 1114112 | tf_op jit(solution)/shard_map/all_to_all | solution.py:18
  12.7 0.0 copy-done
  12.7 11.2 %all-gather.row_ref = bf16[1536,128]{1,0:T(8,128)(2,1)S(1)} all-gather(bf16[384,128]{1,0:T(8,128)(2,1)S(1)} %copy-done), channel_id=2, replica_groups=mesh['y'=8,'core'=2,'x'=4,'z_pair'=4,'z_end'=2] {'x'}, dimensions={0}, use_global_device_ids=true | all-gather | bytes 491520 | tf_op jit(solution)/shard_map/all_gather | solution.py:107
  23.9 4.5 %all-gather.1 = bf16[8,112,128]{2,1,0:T(8,128)(2,1)S(1)} all-gather(bf16[4,112,128]{2,1,0:T(8,128)(2,1)S(1)} %slice.32), channel_id=3, replica_groups=mesh['y'=8,'core'=2,'x'=4,'z_pair'=4,'z_end'=2] {'z_end'}, dimensions={0}, use_global_device_ids=true | all-gather | bytes 344064 | tf_op jit(solution)/shard_map/all_gather | solution.py:108
  28.5 2.9 %all-to-all-done = bf16[8,272,128]{2,1,0:T(8,128)(2,1)S(1)} async-done(((bf16[8,272,128]{2,1,0:T(8,128)(2,1)}), bf16[8,272,128]{2,1,0:T(8,128)(2,1)S(1)}, u32[]{:S(2)}, u32[]{:S(2)}) %all-to-all-start) | async-done | bytes 557088 | tf_op jit(solution)/shard_map/all_to_all | solution.py:18
  31.4 1.5 broadcast_in_dim.17
  33.0 0.0 copy-start.2
  33.0 0.0 copy-start.3
  33.0 4.1 %all-to-all-start.1 = ((bf16[4,7,272,128]{3,2,1,0:T(8,128)(2,1)}), bf16[4,7,272,128]{3,2,1,0:T(8,128)(2,1)S(1)}, u32[]{:S(2)}, u32[]{:S(2)}) async-start(bf16[4,7,272,128]{3,2,1,0:T(8,128)(2,1)} %broadcast_in_dim.17), calls=%async_computation.1 | async-start | bytes 3899392 | tf_op jit(solution)/shard_map/all_to_all | solution.py:18
  37.1 0.0 copy-done.2
  37.2 0.0 copy-done.3
  37.2 17.6 %all-gather.2 = bf16[8,4,112,128]{3,2,1,0:T(8,128)(2,1)S(1)} all-gather(bf16[2,4,112,128]{3,2,1,0:T(8,128)(2,1)S(1)} %bitcast.57), channel_id=4, replica_groups=mesh['y'=8,'core'=2,'x'=4,'z_pair'=4,'z_end'=2] {'z_pair'}, dimensions={0}, use_global_device_ids=true | all-gather | bytes 1146880 | tf_op jit(solution)/shard_map/all_gather | solution.py:112
  54.8 6.2 %all-to-all-done.1 = bf16[4,7,272,128]{3,2,1,0:T(8,128)(2,1)S(1)} async-done(((bf16[4,7,272,128]{3,2,1,0:T(8,128)(2,1)}), bf16[4,7,272,128]{3,2,1,0:T(8,128)(2,1)S(1)}, u32[]{:S(2)}, u32[]{:S(2)}) %all-to-all-start.1) | async-done | bytes 1949728 | tf_op jit(solution)/shard_map/all_to_all | solution.py:18
  61.1 5.0 %shard_map.46 = (f32[24,128,128]{2,1,0:T(8,128)S(1)}, bf16[24,128,128]{2,1,0:T(8,128)(2,1)S(1)}) custom-call(s32[7,128]{1,0:T(8,128)S(1)} %stack.2.slots_ref, bf16[128,128,128]{2,1,0:T(8,128)(2,1)} %bitcast.53, bf16[1536,128]{1,0:T(8,128)(2,1)S(1)} %all-gather.row_ref, bf16[32,112,128]{2,1,0:T(8,128)(2,1)S(1)} %bitcast.50, bf16[7616,128]{1,0:T(8,128)(2,1)S(1)} %bitcast.47), custom_call_target="tpu_custom_call" | custom-call | flops 536870912 | bytes 9420800 | tf_op jit(solution)/shard_map/pallas_call | solution.py:58
  66.1 3.7 %collective-permute-start = (bf16[24,128,128]{2,1,0:T(8,128)(2,1)S(1)}, bf16[24,128,128]{2,1,0:T(8,128)(2,1)S(1)}, u32[]{:S(2)}, u32[]{:S(2)}) collective-permute-start(bf16[24,128,128]{2,1,0:T(8,128)(2,1)S(1)} %get-tuple-element.16), channel_id=1, source_target_pairs={{0,32},{32,0},{1,33},{33,1},{2,34},{34,2},{3,35},{35,3},{4,36},{36... | collective-permute-start | bytes 2359304 | tf_op jit(solution)/shard_map/ppermute | solution.py:114
  69.8 1.9 %collective-permute-done = bf16[24,128,128]{2,1,0:T(8,128)(2,1)S(1)} collective-permute-done((bf16[24,128,128]{2,1,0:T(8,128)(2,1)S(1)}, bf16[24,128,128]{2,1,0:T(8,128)(2,1)S(1)}, u32[]{:S(2)}, u32[]{:S(2)}) %collective-permute-start) | collective-permute-done | bytes 786464 | tf_op jit(solution)/shard_map/ppermute | solution.py:114
  71.7 0.2 add_convert_fusion.1
  71.9 28.9 %all_to_all.30 = bf16[8,384,128]{2,1,0:T(8,128)(2,1)S(1)} all-to-all(bf16[8,384,128]{2,1,0:T(8,128)(2,1)S(1)} %bitcast.55), channel_id=1, replica_groups=mesh['y'=8,'core'=2,'x'=4,'z_pair'=4,'z_end'=2] {'y'}, dimensions={0} | all-to-all | bytes 1572864 | tf_op jit(solution)/shard_map/all_to_all | solution.py:116
  100.8 0.1 reduce_sum.24
  101.0 0.9 broadcast_in_dim.18
  101.9 3.5 %all-to-all-start.3 = ((bf16[8,272,128]{2,1,0:T(8,128)(2,1)}), bf16[8,272,128]{2,1,0:T(8,128)(2,1)S(1)}, u32[]{:S(2)}, u32[]{:S(2)}) async-start(bf16[8,272,128]{2,1,0:T(8,128)(2,1)} %broadcast_in_dim.18), calls=%async_computation.3 | async-start | bytes 1114112 | tf_op jit(solution)/shard_map/all_to_all | solution.py:18
  105.4 10.4 %all-gather.3.row_ref = bf16[1536,128]{1,0:T(8,128)(2,1)S(1)} all-gather(bf16[384,128]{1,0:T(8,128)(2,1)S(1)} %reduce_sum.24), channel_id=5, replica_groups=mesh['y'=8,'core'=2,'x'=4,'z_pair'=4,'z_end'=2] {'x'}, dimensions={0}, use_global_device_ids=true | all-gather | bytes 491520 | tf_op jit(solution)/shard_map/all_gather | solution.py:107
  115.8 5.3 %all-gather.4 = bf16[8,112,128]{2,1,0:T(8,128)(2,1)} all-gather(bf16[4,112,128]{2,1,0:T(8,128)(2,1)S(1)} %slice.35), channel_id=6, replica_groups=mesh['y'=8,'core'=2,'x'=4,'z_pair'=4,'z_end'=2] {'z_end'}, dimensions={0}, use_global_device_ids=true | all-gather | bytes 344064 | tf_op jit(solution)/shard_map/all_gather | solution.py:108
  121.2 0.7 all-to-all-done.3
  121.9 1.5 broadcast_in_dim.19
  123.5 3.6 %all-to-all-start.4 = ((bf16[4,7,272,128]{3,2,1,0:T(8,128)(2,1)}), bf16[4,7,272,128]{3,2,1,0:T(8,128)(2,1)S(1)}, u32[]{:S(2)}, u32[]{:S(2)}) async-start(bf16[4,7,272,128]{3,2,1,0:T(8,128)(2,1)} %broadcast_in_dim.19), calls=%async_computation.4 | async-start | bytes 3899392 | tf_op jit(solution)/shard_map/all_to_all | solution.py:18
  127.1 18.8 %all-gather.5 = bf16[8,4,112,128]{3,2,1,0:T(8,128)(2,1)S(1)} all-gather(bf16[2,4,112,128]{3,2,1,0:T(8,128)(2,1)} %bitcast.58), channel_id=7, replica_groups=mesh['y'=8,'core'=2,'x'=4,'z_pair'=4,'z_end'=2] {'z_pair'}, dimensions={0}, use_global_device_ids=true | all-gather | bytes 1146880 | tf_op jit(solution)/shard_map/all_gather | solution.py:112
  145.9 2.2 %all-to-all-done.4 = bf16[4,7,272,128]{3,2,1,0:T(8,128)(2,1)S(1)} async-done(((bf16[4,7,272,128]{3,2,1,0:T(8,128)(2,1)}), bf16[4,7,272,128]{3,2,1,0:T(8,128)(2,1)S(1)}, u32[]{:S(2)}, u32[]{:S(2)}) %all-to-all-start.4) | async-done | bytes 1949728 | tf_op jit(solution)/shard_map/all_to_all | solution.py:18
  148.2 5.0 %shard_map.47 = (f32[24,128,128]{2,1,0:T(8,128)S(1)}, bf16[24,128,128]{2,1,0:T(8,128)(2,1)S(1)}) custom-call(s32[7,128]{1,0:T(8,128)S(1)} %stack.2.slots_ref, bf16[128,128,128]{2,1,0:T(8,128)(2,1)} %bitcast.54, bf16[1536,128]{1,0:T(8,128)(2,1)S(1)} %all-gather.3.row_ref, bf16[32,112,128]{2,1,0:T(8,128)(2,1)S(1)} %bitcast.49, bf16[7616,128]{1,0:T(8,128)(2,1)S(1)} %bitcast.48), custom_call_target="tpu_custom_call" | custom-call | flops 536870912 | bytes 9420800 | tf_op jit(solution)/shard_map/pallas_call | solution.py:58
  153.2 6.5 %collective-permute-start.1 = (bf16[24,128,128]{2,1,0:T(8,128)(2,1)S(1)}, bf16[24,128,128]{2,1,0:T(8,128)(2,1)S(1)}, u32[]{:S(2)}, u32[]{:S(2)}) collective-permute-start(bf16[24,128,128]{2,1,0:T(8,128)(2,1)S(1)} %get-tuple-element.20), channel_id=1, source_target_pairs={{0,32},{32,0},{1,33},{33,1},{2,34},{34,2},{3,35},{35,3},{4,36},{36... | collective-permute-start | bytes 2359304 | tf_op jit(solution)/shard_map/ppermute | solution.py:114
  159.7 1.9 %collective-permute-done.1 = bf16[24,128,128]{2,1,0:T(8,128)(2,1)S(1)} collective-permute-done((bf16[24,128,128]{2,1,0:T(8,128)(2,1)S(1)}, bf16[24,128,128]{2,1,0:T(8,128)(2,1)S(1)}, u32[]{:S(2)}, u32[]{:S(2)}) %collective-permute-start.1) | collective-permute-done | bytes 786464 | tf_op jit(solution)/shard_map/ppermute | solution.py:114
  161.6 0.2 add_convert_fusion
  161.8 0.0 copy-start.1
  161.9 25.4 %all_to_all.31 = bf16[8,384,128]{2,1,0:T(8,128)(2,1)S(1)} all-to-all(bf16[8,384,128]{2,1,0:T(8,128)(2,1)S(1)} %bitcast.56), channel_id=1, replica_groups=mesh['y'=8,'core'=2,'x'=4,'z_pair'=4,'z_end'=2] {'y'}, dimensions={0} | all-to-all | bytes 1572864 | tf_op jit(solution)/shard_map/all_to_all | solution.py:116
  187.3 0.1 reduce_sum.25
  187.4 0.0 copy-done.1
  187.4 0.7 add_convert_fusion.2
  (14 shorter events, 0.2 us)
Async XLA Ops:
  0.0 12.7 %copy-start = (bf16[384,128]{1,0:T(8,128)(2,1)S(1)}, bf16[384,128]{1,0:T(8,128)(2,1)}, u32[]{:S(2)}) copy-start(bf16[384,128]{1,0:T(8,128)(2,1)} %param.4) | copy-start | bytes 294916
  1.8 29.5 %all-to-all-start = ((bf16[8,272,128]{2,1,0:T(8,128)(2,1)}), bf16[8,272,128]{2,1,0:T(8,128)(2,1)S(1)}, u32[]{:S(2)}, u32[]{:S(2)}) async-start(bf16[8,272,128]{2,1,0:T(8,128)(2,1)} %broadcast_in_dim.16), calls=%async_computation | async-start | bytes 1114112 | tf_op jit(solution)/shard_map/all_to_all | solution.py:18
  33.0 4.2 %copy-start.2 = (s32[1,1,128]{2,1,0:T(1,128)S(1)}, s32[1,1,128]{2,1,0:T(1,128)}, u32[]{:S(2)}) copy-start(s32[1,1,128]{2,1,0:T(1,128)} %param.7) | copy-start | bytes 1540
  33.0 4.2 %copy-start.3 = (s32[1,1,128]{2,1,0:T(1,128)S(1)}, s32[1,1,128]{2,1,0:T(1,128)}, u32[]{:S(2)}) copy-start(s32[1,1,128]{2,1,0:T(1,128)} %param.6) | copy-start | bytes 1540
  33.0 28.1 %all-to-all-start.1 = ((bf16[4,7,272,128]{3,2,1,0:T(8,128)(2,1)}), bf16[4,7,272,128]{3,2,1,0:T(8,128)(2,1)S(1)}, u32[]{:S(2)}, u32[]{:S(2)}) async-start(bf16[4,7,272,128]{3,2,1,0:T(8,128)(2,1)} %broadcast_in_dim.17), calls=%async_computation.1 | async-start | bytes 3899392 | tf_op jit(solution)/shard_map/all_to_all | solution.py:18
  66.1 5.6 %collective-permute-start = (bf16[24,128,128]{2,1,0:T(8,128)(2,1)S(1)}, bf16[24,128,128]{2,1,0:T(8,128)(2,1)S(1)}, u32[]{:S(2)}, u32[]{:S(2)}) collective-permute-start(bf16[24,128,128]{2,1,0:T(8,128)(2,1)S(1)} %get-tuple-element.16), channel_id=1, source_target_pairs={{0,32},{32,0},{1,33},{33,1},{2,34},{34,2},{3,35},{35,3},{4,36},{36... | collective-permute-start | bytes 2359304 | tf_op jit(solution)/shard_map/ppermute | solution.py:114
  101.9 20.0 %all-to-all-start.3 = ((bf16[8,272,128]{2,1,0:T(8,128)(2,1)}), bf16[8,272,128]{2,1,0:T(8,128)(2,1)S(1)}, u32[]{:S(2)}, u32[]{:S(2)}) async-start(bf16[8,272,128]{2,1,0:T(8,128)(2,1)} %broadcast_in_dim.18), calls=%async_computation.3 | async-start | bytes 1114112 | tf_op jit(solution)/shard_map/all_to_all | solution.py:18
  123.5 24.7 %all-to-all-start.4 = ((bf16[4,7,272,128]{3,2,1,0:T(8,128)(2,1)}), bf16[4,7,272,128]{3,2,1,0:T(8,128)(2,1)S(1)}, u32[]{:S(2)}, u32[]{:S(2)}) async-start(bf16[4,7,272,128]{3,2,1,0:T(8,128)(2,1)} %broadcast_in_dim.19), calls=%async_computation.4 | async-start | bytes 3899392 | tf_op jit(solution)/shard_map/all_to_all | solution.py:18
  153.2 8.4 %collective-permute-start.1 = (bf16[24,128,128]{2,1,0:T(8,128)(2,1)S(1)}, bf16[24,128,128]{2,1,0:T(8,128)(2,1)S(1)}, u32[]{:S(2)}, u32[]{:S(2)}) collective-permute-start(bf16[24,128,128]{2,1,0:T(8,128)(2,1)S(1)} %get-tuple-element.20), channel_id=1, source_target_pairs={{0,32},{32,0},{1,33},{33,1},{2,34},{34,2},{3,35},{35,3},{4,36},{36... | collective-permute-start | bytes 2359304 | tf_op jit(solution)/shard_map/ppermute | solution.py:114
  161.8 25.5 %copy-start.1 = (bf16[384,128]{1,0:T(8,128)(2,1)S(1)}, bf16[384,128]{1,0:T(8,128)(2,1)}, u32[]{:S(2)}) copy-start(bf16[384,128]{1,0:T(8,128)(2,1)} %param.4) | copy-start | bytes 294916

commit v5 on v4

--- a/solution.py
+++ b/solution.py
@@ -9,7 +9,7 @@
 Z = ("z_pair", "z_end")
 COL = ("x", *Z)
 ROW_COL = ("y", "core", *COL)
-CHUNK = 16
+CHUNK = 32
 EARLY = 112
 
 
@@ -18,9 +18,9 @@
     return lax.all_to_all(copies, axis, split_axis=0, concat_axis=0, tiled=True)
 
 
-def tile_kernel(slots_ref, tiles_hbm_ref, row_ref, early_ref, late_ref, keep_ref, send_ref, tiles_ref, total_ref, sems):
+def tile_kernel(slots_ref, tiles_hbm_ref, row_ref, early_ref, late_ref, total_ref, send_ref, tiles_ref, sems):
     edge = tiles_ref.shape[-1]
-    half = keep_ref.shape[0]
+    half = send_ref.shape[0]
 
     def fetch(step):
         at = pl.ds(step * CHUNK, CHUNK)
@@ -48,7 +48,6 @@
         for k, product in enumerate(products):
             total_ref[slots_ref[0, step * CHUNK + k]] += product
 
-    keep_ref[...] = total_ref[:half].astype(keep_ref.dtype)
     send_ref[...] = total_ref[half : 2 * half].astype(send_ref.dtype)
 
 
@@ -58,14 +57,13 @@
     return pl.pallas_call(
         tile_kernel,
         out_shape=[
-            jax.ShapeDtypeStruct((half, edge, columns), jnp.float32),
+            jax.ShapeDtypeStruct((2 * half + 1, edge, columns), jnp.float32),
             jax.ShapeDtypeStruct((half, edge, columns), jnp.bfloat16),
         ],
         in_specs=[pl.BlockSpec(memory_space=pltpu.SMEM), pl.BlockSpec(memory_space=pl.ANY), vmem, vmem, vmem],
         out_specs=[vmem, vmem],
         scratch_shapes=[
             pltpu.VMEM(tiles.shape, tiles.dtype),
-            pltpu.VMEM((2 * half + 1, edge, columns), jnp.float32),
             pltpu.SemaphoreType.DMA((tiles.shape[0] // CHUNK,)),
         ],
         compiler_params=pltpu.CompilerParams(vmem_limit_bytes=24 << 20),
@@ -110,9 +108,9 @@
         others = lax.dynamic_update_index_in_dim(late_line, late_line[-1], my_z, 0)[:-1]
         late_panel = spread(others, "x")
         early_panel = lax.all_gather(early_pair, "z_pair")
-        keep, send = tile_products(slots, tile_block, row, early_panel, late_panel, half)
+        total, send = tile_products(slots, tile_block, row, early_panel, late_panel, half)
         other = lax.ppermute(send, "core", [(0, 1), (1, 0)])
-        both = (keep + other.astype(jnp.float32)).astype(jnp.bfloat16)
+        both = (total[:half] + other.astype(jnp.float32)).astype(jnp.bfloat16)
         arrived = lax.all_to_all(
             both.reshape(chips, -1, columns), "y", split_axis=0, concat_axis=0, tiled=True
         )

time: 189 us -> 188 us (level)
  no operation moved by 1% of the time
where the time goes in v5:
time: 188 us; the launch traced here: 187 us
  blocking collectives  123 us (65%)
  starting transfers between devices  32.3 us (17%)
  waiting for transfers between devices  15.5 us (8%)
  Pallas kernels  9.22 us (5%)
  local copies, waits for them, and re-layouts  5.98 us (3%)
    all_to_all x2, blocking collectives, multiply(): lax.all_to_all(both.reshape(chips, -1, columns), 'y', split_axis=0, conca...  54.4 us
    all_gather x2, blocking collectives, multiply(): early_panel = lax.all_gather(early_pair, 'z_pair')  36.8 us
    all_to_all x4, starting transfers between devices, spread(): return lax.all_to_all(copies, axis, split_axis=0, concat_axis=0, tiled=True)  22.1 us
    all_gather x2, blocking collectives, multiply(): row = lax.all_gather(piece, 'x')  21.6 us
    all_to_all x4, waiting for transfers between devices, spread(): return lax.all_to_all(copies, axis, split_axis=0, concat_axis=0, tiled=True)  11.7 us
    ppermute x2, starting transfers between devices, multiply(): other = lax.ppermute(send, 'core', [(0, 1), (1, 0)])  10.1 us
    all_gather x2, blocking collectives, multiply(): early_pair = lax.all_gather(row[:, :EARLY], 'z_end')  9.89 us
    pallas_call x2, Pallas kernels, tile_products(): pl.pallas_call(tile_kernel, out_shape=[jax.ShapeDtypeStruct((2 * half + 1...  9.22 us
  transfers between devices with their start and end apart: 6, of which 6 were waited for; matrix products, arithmetic and copies ran while one was open for 0% of the time, Pallas kernels for 0%

profile of v5, /device:TPU:1, one launch (start us, length us, event | category | flops | bytes accessed | tf_op | source)
XLA Modules:
  0.0 187.3 jit_solution(14238937824648631400)
XLA Ops:
  0.0 0.0 copy-start
  0.0 1.0 slice.30
  1.0 0.9 broadcast_in_dim.16
  1.8 10.9 %all-to-all-start = ((bf16[8,272,128]{2,1,0:T(8,128)(2,1)}), bf16[8,272,128]{2,1,0:T(8,128)(2,1)S(1)}, u32[]{:S(2)}, u32[]{:S(2)}) async-start(bf16[8,272,128]{2,1,0:T(8,128)(2,1)} %broadcast_in_dim.16), calls=%async_computation | async-start | bytes 1114112 | tf_op jit(solution)/shard_map/all_to_all | solution.py:18
  12.7 0.0 copy-done
  12.7 11.2 %all-gather.row_ref = bf16[1536,128]{1,0:T(8,128)(2,1)S(1)} all-gather(bf16[384,128]{1,0:T(8,128)(2,1)S(1)} %copy-done), channel_id=2, replica_groups=mesh['y'=8,'core'=2,'x'=4,'z_pair'=4,'z_end'=2] {'x'}, dimensions={0}, use_global_device_ids=true | all-gather | bytes 491520 | tf_op jit(solution)/shard_map/all_gather | solution.py:105
  23.9 4.5 %all-gather.1 = bf16[8,112,128]{2,1,0:T(8,128)(2,1)S(1)} all-gather(bf16[4,112,128]{2,1,0:T(8,128)(2,1)S(1)} %slice.40), channel_id=3, replica_groups=mesh['y'=8,'core'=2,'x'=4,'z_pair'=4,'z_end'=2] {'z_end'}, dimensions={0}, use_global_device_ids=true | all-gather | bytes 344064 | tf_op jit(solution)/shard_map/all_gather | solution.py:106
  28.5 2.9 %all-to-all-done = bf16[8,272,128]{2,1,0:T(8,128)(2,1)S(1)} async-done(((bf16[8,272,128]{2,1,0:T(8,128)(2,1)}), bf16[8,272,128]{2,1,0:T(8,128)(2,1)S(1)}, u32[]{:S(2)}, u32[]{:S(2)}) %all-to-all-start) | async-done | bytes 557088 | tf_op jit(solution)/shard_map/all_to_all | solution.py:18
  31.4 1.5 broadcast_in_dim.17
  33.0 0.0 copy-start.2
  33.0 0.0 copy-start.3
  33.0 4.1 %all-to-all-start.1 = ((bf16[4,7,272,128]{3,2,1,0:T(8,128)(2,1)}), bf16[4,7,272,128]{3,2,1,0:T(8,128)(2,1)S(1)}, u32[]{:S(2)}, u32[]{:S(2)}) async-start(bf16[4,7,272,128]{3,2,1,0:T(8,128)(2,1)} %broadcast_in_dim.17), calls=%async_computation.1 | async-start | bytes 3899392 | tf_op jit(solution)/shard_map/all_to_all | solution.py:18
  37.1 0.0 copy-done.2
  37.2 0.0 copy-done.3
  37.2 17.6 %all-gather.2 = bf16[8,4,112,128]{3,2,1,0:T(8,128)(2,1)S(1)} all-gather(bf16[2,4,112,128]{3,2,1,0:T(8,128)(2,1)S(1)} %bitcast.57), channel_id=4, replica_groups=mesh['y'=8,'core'=2,'x'=4,'z_pair'=4,'z_end'=2] {'z_pair'}, dimensions={0}, use_global_device_ids=true | all-gather | bytes 1146880 | tf_op jit(solution)/shard_map/all_gather | solution.py:110
  54.8 6.2 %all-to-all-done.1 = bf16[4,7,272,128]{3,2,1,0:T(8,128)(2,1)S(1)} async-done(((bf16[4,7,272,128]{3,2,1,0:T(8,128)(2,1)}), bf16[4,7,272,128]{3,2,1,0:T(8,128)(2,1)S(1)}, u32[]{:S(2)}, u32[]{:S(2)}) %all-to-all-start.1) | async-done | bytes 1949728 | tf_op jit(solution)/shard_map/all_to_all | solution.py:18
  61.1 4.6 %shard_map.46 = (f32[49,128,128]{2,1,0:T(8,128)S(1)}, bf16[24,128,128]{2,1,0:T(8,128)(2,1)S(1)}) custom-call(s32[7,128]{1,0:T(8,128)S(1)} %stack.2.slots_ref, bf16[128,128,128]{2,1,0:T(8,128)(2,1)} %bitcast.53, bf16[1536,128]{1,0:T(8,128)(2,1)S(1)} %all-gather.row_ref, bf16[32,112,128]{2,1,0:T(8,128)(2,1)S(1)} %bitcast.50, bf16[7616,128]{1,0:T(8,128)(2,1)S(1)} %bitcast.47), custom_call_target="tpu_custom_call" | custom-call | flops 536870912 | bytes 9420800 | tf_op jit(solution)/shard_map/pallas_call | solution.py:57
  65.7 3.7 %collective-permute-start = (bf16[24,128,128]{2,1,0:T(8,128)(2,1)S(1)}, bf16[24,128,128]{2,1,0:T(8,128)(2,1)S(1)}, u32[]{:S(2)}, u32[]{:S(2)}) collective-permute-start(bf16[24,128,128]{2,1,0:T(8,128)(2,1)S(1)} %get-tuple-element.16), channel_id=1, source_target_pairs={{0,32},{32,0},{1,33},{33,1},{2,34},{34,2},{3,35},{35,3},{4,36},{36... | collective-permute-start | bytes 2359304 | tf_op jit(solution)/shard_map/ppermute | solution.py:112
  69.4 1.9 %collective-permute-done = bf16[24,128,128]{2,1,0:T(8,128)(2,1)S(1)} collective-permute-done((bf16[24,128,128]{2,1,0:T(8,128)(2,1)S(1)}, bf16[24,128,128]{2,1,0:T(8,128)(2,1)S(1)}, u32[]{:S(2)}, u32[]{:S(2)}) %collective-permute-start) | collective-permute-done | bytes 786464 | tf_op jit(solution)/shard_map/ppermute | solution.py:112
  71.2 0.2 add_convert_fusion.1
  71.5 29.0 %all_to_all.30 = bf16[8,384,128]{2,1,0:T(8,128)(2,1)S(1)} all-to-all(bf16[8,384,128]{2,1,0:T(8,128)(2,1)S(1)} %bitcast.55), channel_id=1, replica_groups=mesh['y'=8,'core'=2,'x'=4,'z_pair'=4,'z_end'=2] {'y'}, dimensions={0} | all-to-all | bytes 1572864 | tf_op jit(solution)/shard_map/all_to_all | solution.py:114
  100.4 0.1 reduce_sum.24
  100.6 0.9 broadcast_in_dim.18
  101.5 3.5 %all-to-all-start.3 = ((bf16[8,272,128]{2,1,0:T(8,128)(2,1)}), bf16[8,272,128]{2,1,0:T(8,128)(2,1)S(1)}, u32[]{:S(2)}, u32[]{:S(2)}) async-start(bf16[8,272,128]{2,1,0:T(8,128)(2,1)} %broadcast_in_dim.18), calls=%async_computation.3 | async-start | bytes 1114112 | tf_op jit(solution)/shard_map/all_to_all | solution.py:18
  105.0 10.4 %all-gather.3.row_ref = bf16[1536,128]{1,0:T(8,128)(2,1)S(1)} all-gather(bf16[384,128]{1,0:T(8,128)(2,1)S(1)} %reduce_sum.24), channel_id=5, replica_groups=mesh['y'=8,'core'=2,'x'=4,'z_pair'=4,'z_end'=2] {'x'}, dimensions={0}, use_global_device_ids=true | all-gather | bytes 491520 | tf_op jit(solution)/shard_map/all_gather | solution.py:105
  115.4 5.4 %all-gather.4 = bf16[8,112,128]{2,1,0:T(8,128)(2,1)} all-gather(bf16[4,112,128]{2,1,0:T(8,128)(2,1)S(1)} %slice.43), channel_id=6, replica_groups=mesh['y'=8,'core'=2,'x'=4,'z_pair'=4,'z_end'=2] {'z_end'}, dimensions={0}, use_global_device_ids=true | all-gather | bytes 344064 | tf_op jit(solution)/shard_map/all_gather | solution.py:106
  120.8 0.7 all-to-all-done.3
  121.5 1.5 broadcast_in_dim.19
  123.1 3.6 %all-to-all-start.4 = ((bf16[4,7,272,128]{3,2,1,0:T(8,128)(2,1)}), bf16[4,7,272,128]{3,2,1,0:T(8,128)(2,1)S(1)}, u32[]{:S(2)}, u32[]{:S(2)}) async-start(bf16[4,7,272,128]{3,2,1,0:T(8,128)(2,1)} %broadcast_in_dim.19), calls=%async_computation.4 | async-start | bytes 3899392 | tf_op jit(solution)/shard_map/all_to_all | solution.py:18
  126.7 19.2 %all-gather.5 = bf16[8,4,112,128]{3,2,1,0:T(8,128)(2,1)S(1)} all-gather(bf16[2,4,112,128]{3,2,1,0:T(8,128)(2,1)} %bitcast.58), channel_id=7, replica_groups=mesh['y'=8,'core'=2,'x'=4,'z_pair'=4,'z_end'=2] {'z_pair'}, dimensions={0}, use_global_device_ids=true | all-gather | bytes 1146880 | tf_op jit(solution)/shard_map/all_gather | solution.py:110
  145.9 1.9 %all-to-all-done.4 = bf16[4,7,272,128]{3,2,1,0:T(8,128)(2,1)S(1)} async-done(((bf16[4,7,272,128]{3,2,1,0:T(8,128)(2,1)}), bf16[4,7,272,128]{3,2,1,0:T(8,128)(2,1)S(1)}, u32[]{:S(2)}, u32[]{:S(2)}) %all-to-all-start.4) | async-done | bytes 1949728 | tf_op jit(solution)/shard_map/all_to_all | solution.py:18
  147.8 4.6 %shard_map.47 = (f32[49,128,128]{2,1,0:T(8,128)S(1)}, bf16[24,128,128]{2,1,0:T(8,128)(2,1)S(1)}) custom-call(s32[7,128]{1,0:T(8,128)S(1)} %stack.2.slots_ref, bf16[128,128,128]{2,1,0:T(8,128)(2,1)} %bitcast.54, bf16[1536,128]{1,0:T(8,128)(2,1)S(1)} %all-gather.3.row_ref, bf16[32,112,128]{2,1,0:T(8,128)(2,1)S(1)} %bitcast.49, bf16[7616,128]{1,0:T(8,128)(2,1)S(1)} %bitcast.48), custom_call_target="tpu_custom_call" | custom-call | flops 536870912 | bytes 9420800 | tf_op jit(solution)/shard_map/pallas_call | solution.py:57
  152.4 6.5 %collective-permute-start.1 = (bf16[24,128,128]{2,1,0:T(8,128)(2,1)S(1)}, bf16[24,128,128]{2,1,0:T(8,128)(2,1)S(1)}, u32[]{:S(2)}, u32[]{:S(2)}) collective-permute-start(bf16[24,128,128]{2,1,0:T(8,128)(2,1)S(1)} %get-tuple-element.20), channel_id=1, source_target_pairs={{0,32},{32,0},{1,33},{33,1},{2,34},{34,2},{3,35},{35,3},{4,36},{36... | collective-permute-start | bytes 2359304 | tf_op jit(solution)/shard_map/ppermute | solution.py:112
  158.9 1.9 %collective-permute-done.1 = bf16[24,128,128]{2,1,0:T(8,128)(2,1)S(1)} collective-permute-done((bf16[24,128,128]{2,1,0:T(8,128)(2,1)S(1)}, bf16[24,128,128]{2,1,0:T(8,128)(2,1)S(1)}, u32[]{:S(2)}, u32[]{:S(2)}) %collective-permute-start.1) | collective-permute-done | bytes 786464 | tf_op jit(solution)/shard_map/ppermute | solution.py:112
  160.8 0.2 add_convert_fusion
  161.0 0.0 copy-start.1
  161.0 25.4 %all_to_all.31 = bf16[8,384,128]{2,1,0:T(8,128)(2,1)S(1)} all-to-all(bf16[8,384,128]{2,1,0:T(8,128)(2,1)S(1)} %bitcast.56), channel_id=1, replica_groups=mesh['y'=8,'core'=2,'x'=4,'z_pair'=4,'z_end'=2] {'y'}, dimensions={0} | all-to-all | bytes 1572864 | tf_op jit(solution)/shard_map/all_to_all | solution.py:114
  186.5 0.1 reduce_sum.25
  186.6 0.0 copy-done.1
  186.6 0.7 add_convert_fusion.2
  (14 shorter events, 0.2 us)
Async XLA Ops:
  0.0 12.7 %copy-start = (bf16[384,128]{1,0:T(8,128)(2,1)S(1)}, bf16[384,128]{1,0:T(8,128)(2,1)}, u32[]{:S(2)}) copy-start(bf16[384,128]{1,0:T(8,128)(2,1)} %param.4) | copy-start | bytes 294916
  1.8 29.5 %all-to-all-start = ((bf16[8,272,128]{2,1,0:T(8,128)(2,1)}), bf16[8,272,128]{2,1,0:T(8,128)(2,1)S(1)}, u32[]{:S(2)}, u32[]{:S(2)}) async-start(bf16[8,272,128]{2,1,0:T(8,128)(2,1)} %broadcast_in_dim.16), calls=%async_computation | async-start | bytes 1114112 | tf_op jit(solution)/shard_map/all_to_all | solution.py:18
  33.0 4.2 %copy-start.2 = (s32[1,1,128]{2,1,0:T(1,128)S(1)}, s32[1,1,128]{2,1,0:T(1,128)}, u32[]{:S(2)}) copy-start(s32[1,1,128]{2,1,0:T(1,128)} %param.7) | copy-start | bytes 1540
  33.0 4.2 %copy-start.3 = (s32[1,1,128]{2,1,0:T(1,128)S(1)}, s32[1,1,128]{2,1,0:T(1,128)}, u32[]{:S(2)}) copy-start(s32[1,1,128]{2,1,0:T(1,128)} %param.6) | copy-start | bytes 1540
  33.0 28.1 %all-to-all-start.1 = ((bf16[4,7,272,128]{3,2,1,0:T(8,128)(2,1)}), bf16[4,7,272,128]{3,2,1,0:T(8,128)(2,1)S(1)}, u32[]{:S(2)}, u32[]{:S(2)}) async-start(bf16[4,7,272,128]{3,2,1,0:T(8,128)(2,1)} %broadcast_in_dim.17), calls=%async_computation.1 | async-start | bytes 3899392 | tf_op jit(solution)/shard_map/all_to_all | solution.py:18
  65.7 5.6 %collective-permute-start = (bf16[24,128,128]{2,1,0:T(8,128)(2,1)S(1)}, bf16[24,128,128]{2,1,0:T(8,128)(2,1)S(1)}, u32[]{:S(2)}, u32[]{:S(2)}) collective-permute-start(bf16[24,128,128]{2,1,0:T(8,128)(2,1)S(1)} %get-tuple-element.16), channel_id=1, source_target_pairs={{0,32},{32,0},{1,33},{33,1},{2,34},{34,2},{3,35},{35,3},{4,36},{36... | collective-permute-start | bytes 2359304 | tf_op jit(solution)/shard_map/ppermute | solution.py:112
  101.5 20.0 %all-to-all-start.3 = ((bf16[8,272,128]{2,1,0:T(8,128)(2,1)}), bf16[8,272,128]{2,1,0:T(8,128)(2,1)S(1)}, u32[]{:S(2)}, u32[]{:S(2)}) async-start(bf16[8,272,128]{2,1,0:T(8,128)(2,1)} %broadcast_in_dim.18), calls=%async_computation.3 | async-start | bytes 1114112 | tf_op jit(solution)/shard_map/all_to_all | solution.py:18
  123.1 24.7 %all-to-all-start.4 = ((bf16[4,7,272,128]{3,2,1,0:T(8,128)(2,1)}), bf16[4,7,272,128]{3,2,1,0:T(8,128)(2,1)S(1)}, u32[]{:S(2)}, u32[]{:S(2)}) async-start(bf16[4,7,272,128]{3,2,1,0:T(8,128)(2,1)} %broadcast_in_dim.19), calls=%async_computation.4 | async-start | bytes 3899392 | tf_op jit(solution)/shard_map/all_to_all | solution.py:18
  152.4 8.4 %collective-permute-start.1 = (bf16[24,128,128]{2,1,0:T(8,128)(2,1)S(1)}, bf16[24,128,128]{2,1,0:T(8,128)(2,1)S(1)}, u32[]{:S(2)}, u32[]{:S(2)}) collective-permute-start(bf16[24,128,128]{2,1,0:T(8,128)(2,1)S(1)} %get-tuple-element.20), channel_id=1, source_target_pairs={{0,32},{32,0},{1,33},{33,1},{2,34},{34,2},{3,35},{35,3},{4,36},{36... | collective-permute-start | bytes 2359304 | tf_op jit(solution)/shard_map/ppermute | solution.py:112
  161.0 25.6 %copy-start.1 = (bf16[384,128]{1,0:T(8,128)(2,1)S(1)}, bf16[384,128]{1,0:T(8,128)(2,1)}, u32[]{:S(2)}) copy-start(bf16[384,128]{1,0:T(8,128)(2,1)} %param.4) | copy-start | bytes 294916
